TPU v7x, 32 devices: a whole 2x2x4 slice. The times are simulated.
32 devices in a mesh: cuts: 2 (over core), lx: 2 (over x), ly: 8 (over z, y).
Axes of the slice: x: 2, y: 2, z: 4, core: 2. Of those that a mesh axis runs over, the one named last changes fastest.
Arguments:
- disorder: int32 [16, 16, 128], P('lx', 'ly'), may hold values from 0 to 255
- slice_bounds: float32 [12, 2], P('cuts'), may hold values from -1.5 to 1.5
- start: float32 [12, 32, 16, 16, 128], P('cuts', None, 'lx', 'ly'), may hold values from -36 to 36
- ritz: float32 [12, 8, 16, 16, 128], P('cuts', None, 'lx', 'ly'), may hold values from -4 to 4
Outputs:
- block: float32 [12, 32, 16, 16, 128], P('cuts', None, 'lx', 'ly')
- correlations: float32 [12, 16, 32], P('cuts')
All inputs are finite; a program needn't handle non-finite values.
Results may differ from a plain program's by a relative error of at most 0.000096.
Values sent between devices are 32-bit elements; how exact they have to be, the bound alone decides.
A program may use at most 64 MiB of HBM per device.

v0:
```python
import functools

import jax
import jax.numpy as jnp
from jax import lax
from jax.experimental import pallas as pl
from jax.experimental.pallas import tpu as pltpu
from jax.sharding import PartitionSpec as P

LEVELS = 256
MESH = pl.DeviceIdType.MESH
HP = lax.Precision.HIGHEST
H = 2


def kernel(dims, dis_h, bnd, start_h, ritz_h, out, cor, dis, start, ritz, ls, E, T, O, U, FA, FT, RA, ACC, LM, PK, RX, RZ, SM, AL,
           hs, hr, fs, fr, rs, rr, xs, xr, zs, zr, gs, gr):
    nc, nx, ny, count, NV, NR, X, Y, NZ = dims
    S = count // 2
    CH = E.shape[0] // S
    NC = S * CH
    W = NV // CH
    R = 2 * Y
    J = X * Y
    K = ny // 2
    ng = nx * 2
    tg = RX.shape[1]
    tiles = ng * tg
    total = float(J * NZ * nx * ny)
    cut, mx, my = lax.axis_index("cuts"), lax.axis_index("lx"), lax.axis_index("ly")
    p = lax.rem(my, 2)
    q = 1 - p
    kz = my // 2
    g = mx * 2 + p
    partner = kz * 2 + q
    zup = lax.rem(kz + 1, K) * 2 + p
    zdown = lax.rem(kz + K - 1, K) * 2 + p
    xup = lax.rem(mx + 1, nx)
    xdown = lax.rem(mx + nx - 1, nx)

    def load(src, dst, i):
        copy = pltpu.make_async_copy(src, dst, ls.at[i])
        copy.start()
        return copy

    away = [load(start_h.at[q * S + c], start.at[c], c) for c in range(S)]
    level_load = load(dis_h, dis, 2 * S)
    kept = [load(start_h.at[p * S + c], start.at[S + c], S + c) for c in range(S)]
    ritz_load = load(ritz_h, ritz, 2 * S + 1)
    barrier = pltpu.get_barrier_semaphore()

    def greet(dev):
        pl.semaphore_signal(barrier, inc=1, device_id=dev, device_id_type=MESH)

    def in_plane(o):
        t = lax.rem(g + o, ng)
        return t, (cut, t // 2, kz * 2 + lax.rem(t, 2))

    def in_line(o):
        t = lax.rem(kz + o, K)
        return t, (cut, mx, t * 2 + p)

    for o in range(1, ng):
        greet(in_plane(o)[1])
    for o in range(1, K):
        greet(in_line(o)[1])
    cup = (lax.rem(cut + 1, nc), mx, my)
    cdown = (lax.rem(cut + nc - 1, nc), mx, my)
    greet(cup)
    greet(cdown)

    lo = H + Y * p
    for c in range(NC):
        if c % CH == 0:
            away[c // CH].wait()
        for x in range(X):
            for r in range(Y):
                T[c, x, r] = start[c // CH, pl.ds((c % CH) * W * J + x * Y + r, W, stride=J), :]
    level_load.wait()
    for x in range(X):
        for r in range(Y):
            row = dis[pl.ds(x * Y + r, 1), :].astype(jnp.float32)
            row = 16.5 * (row / jnp.float32(LEVELS - 1) - 0.5)
            O[H + x, lo + r] = jnp.broadcast_to(row, (8, NZ))
    pl.semaphore_wait(barrier, ng + K)

    pending = []

    def send(src, dst, ss, rs_, dev):
        copy = pltpu.make_async_remote_copy(
            src_ref=src, dst_ref=dst, send_sem=ss, recv_sem=rs_, device_id=dev, device_id_type=MESH)
        copy.start()
        pending.append(copy)

    def arrived(dst, rs_):
        pltpu.make_async_remote_copy(
            src_ref=dst, dst_ref=dst, send_sem=rs_, recv_sem=rs_,
            device_id=(cut, mx, partner), device_id_type=MESH).wait_recv()

    fields = [(NC, O)] + [(c, E.at[c]) for c in range(NC)]
    xi = pl.ds(H, X)
    xy = (cut, mx, partner)

    def row_block(at):
        return pl.ds(at, Y)

    def send_rows(c, buf, half):
        up = half
        target = jnp.where(up == 1, zup, zdown)
        dst_row = jnp.where(up == 1, 0, H + R)
        side = 1 - up
        send(buf.at[xi, row_block(H + Y * half)], buf.at[xi, row_block(dst_row)],
             hs.at[c, 1 + side], hr.at[c, 1 + side], (cut, mx, target))

    for c, buf in fields:
        src = buf.at[xi, row_block(lo)] if c == NC else T.at[c]
        send(src, buf.at[xi, row_block(lo)], hs.at[c, 0], hr.at[c, 0], xy)
    for c in range(NC):
        if c % CH == 0:
            kept[c // CH].wait()
        for x in range(X):
            for r in range(Y):
                E[c, H + x, lo + r] = start[S + c // CH, pl.ds((c % CH) * W * J + x * Y + r, W, stride=J), :]
    for c, buf in fields[:2]:
        send_rows(c, buf, p)
    ritz_load.wait()
    for s in range(count):
        for x in range(X):
            for r in range(Y):
                RA[s + 1, x, r] = ritz[s, pl.ds(x * Y + r, NR, stride=J), :]

    own = pl.ds(H, R)
    for c, buf in fields:
        arrived(buf.at[xi, row_block(H + Y * q)], hr.at[c, 0])
        send_rows(c, buf, q)
        if c < NC - 1:
            send_rows(c + 1, fields[c + 2][1], p)
        send(buf.at[pl.ds(X, H), own], buf.at[pl.ds(0, H), own], hs.at[c, 3], hr.at[c, 3], (cut, xup, my))
        send(buf.at[pl.ds(H, H), own], buf.at[pl.ds(H + X, H), own], hs.at[c, 4], hr.at[c, 4], (cut, xdown, my))

    send(RA.at[count], RA.at[0], rs.at[0], rr.at[0], cup)
    send(RA.at[1], RA.at[count + 1], rs.at[1], rr.at[1], cdown)

    def point(src, c, x, r, centre):
        v = src(x, r)
        beside = src(x + 1, r) + src(x - 1, r)
        beside = beside + src(x, r + 1) + src(x, r - 1)
        beside = beside + pltpu.roll(v, 1, 1) + pltpu.roll(v, NZ - 1, 1)
        level = O[x, r] - centre
        level = jnp.concatenate([level] * (W // 8), 0)
        return (level * v - beside) * 0.0625

    for c, buf in fields:
        for side, row in ((0, 0), (1, H + R)):
            arrived(buf.at[xi, row_block(row)], hr.at[c, 1 + side])
        for side, row in ((0, 1), (1, H + R)):
            send(buf.at[H + X - 1, row], buf.at[1, row], hs.at[c, 5 + 2 * side], hr.at[c, 5 + 2 * side], (cut, xup, my))
            send(buf.at[H, row], buf.at[H + X, row], hs.at[c, 6 + 2 * side], hr.at[c, 6 + 2 * side], (cut, xdown, my))
        arrived(buf.at[pl.ds(0, H), own], hr.at[c, 3])
        arrived(buf.at[pl.ds(H + X, H), own], hr.at[c, 4])
        for side, row in ((0, 1), (1, H + R)):
            arrived(buf.at[1, row], hr.at[c, 5 + 2 * side])
            arrived(buf.at[H + X, row], hr.at[c, 6 + 2 * side])
        if c == NC:
            continue
        s = p * S + c // CH
        part = pl.ds((c % CH) * W, W)
        centre = (bnd[0, s] + bnd[1, s]) / 2.0

        def from_e(x, r, c=c):
            return E[c, x, r]

        def from_u(x, r):
            return U[x, r]

        for x in (1, H + X):
            for r in range(H, H + R):
                U[x, r] = point(from_e, c, x, r, centre)

        def first(i, carry, c=c, centre=centre):
            for r in range(1, H + R + 1):
                U[H + i, r] = point(from_e, c, H + i, r, centre)
            return carry

        lax.fori_loop(0, X, first, 0)

        def second(i, carry, c=c, s=s, centre=centre, part=part):
            for r in range(Y):
                a = H + Y * p + r
                FA[s, i, r, part] = 2.0 * point(from_u, c, H + i, a, centre) - E[c, H + i, a]
                b = H + Y * q + r
                FT[c, i, r] = 2.0 * point(from_u, c, H + i, b, centre) - E[c, H + i, b]
            return carry

        lax.fori_loop(0, X, second, 0)
        send(FT.at[c], FA.at[s, :, :, part], fs.at[c], fr.at[c], xy)

    arrived(RA.at[0], rr.at[0])
    arrived(RA.at[count + 1], rr.at[1])

    @pl.when(cut == 0)
    def _():
        RA[0] = jnp.zeros((X, Y, NR, NZ), jnp.float32)

    @pl.when(cut == nc - 1)
    def _():
        RA[count + 1] = jnp.zeros((X, Y, NR, NZ), jnp.float32)

    for c in range(NC):
        arrived(FA.at[q * S + c // CH, :, :, pl.ds((c % CH) * W, W)], fr.at[c])

    contract = (((1,), (1,)), ((), ()))
    ACC[...] = jnp.zeros(ACC.shape, jnp.float32)

    def grams(i, carry):
        z = [jnp.concatenate([FA[s, i, r] for s in range(count)] + [RA[t, i, r] for t in range(count + 2)], 0)
             for r in range(Y)]
        z = jnp.concatenate(z, 1)
        ACC[...] += lax.dot_general(z, z, contract, precision=HP, preferred_element_type=jnp.float32)
        return carry

    lax.fori_loop(0, X, grams, 0)

    NL = ACC.shape[1]
    base = count * NV
    lane = lax.broadcasted_iota(jnp.int32, (8, NL), 1)

    def masked(row, first, width):
        keep = jnp.logical_and(lane >= first, lane < first + width)
        return jnp.where(keep, ACC[pl.ds(row, 8), :], 0.0)

    packed = []
    for b in range(NV // 8):
        acc = jnp.zeros((8, NL), jnp.float32)
        for s in range(count):
            acc = acc + masked(s * NV + b * 8, s * NV, NV)
        if b == 0:
            for t in range(count + 2):
                acc = acc + masked(base + t * NR, base + t * NR, NR)
        if b == 1:
            for s in range(count):
                acc = acc + masked(base + s * NR, base + (s + 2) * NR, NR)
        if b == 2:
            for s in range(count):
                acc = acc + masked(base + (s + 2) * NR, base + s * NR, NR)
        packed.append(acc)
    for b in range(2):
        acc = jnp.zeros((8, NL), jnp.float32)
        for s in range(count):
            acc = acc + masked(base + (s + 2 * b) * NR, s * NV, NV)
        packed.append(acc)
    halves = NL // 128
    used = len(packed) * halves
    for i in range(tiles):
        if i < used:
            h = i % halves
            PK[i] = packed[i // halves][:, h * 128:(h + 1) * 128]
        else:
            PK[i] = jnp.zeros((8, 128), jnp.float32)

    RX[g] = PK[pl.ds(g * tg, tg)]
    for o in range(1, ng):
        t, dev = in_plane(o)
        send(PK.at[pl.ds(t * tg, tg)], RX.at[g], xs.at[o], xr.at[g], dev)
    for o in range(1, ng):
        t, _ = in_plane(o)
        arrived(RX.at[t], xr.at[t])
    mine = RX[0]
    for t in range(1, ng):
        mine = mine + RX[t]
    RZ[kz] = mine
    SM[...] = mine
    for o in range(1, K):
        t, dev = in_line(o)
        send(SM, RZ.at[kz], zs.at[o], zr.at[kz], dev)
    for o in range(1, K):
        t, _ = in_line(o)
        arrived(RZ.at[t], zr.at[t])
    mine = RZ[0]
    for t in range(1, K):
        mine = mine + RZ[t]
    AL[g] = mine
    for o in range(1, ng):
        t, dev = in_plane(o)
        send(AL.at[g], AL.at[g], gs.at[o], gr.at[g], dev)
    for o in range(1, ng):
        t, _ = in_plane(o)
        arrived(AL.at[t], gr.at[t])

    def tile(row, first):
        i = row * halves + first // 128
        value = AL[i // tg, i % tg] * (1.0 / total)
        shift = first % 128
        return pltpu.roll(value, 128 - shift, 1) if shift else value

    l8 = lax.broadcasted_iota(jnp.int32, (8, 128), 1)
    l32 = lax.broadcasted_iota(jnp.int32, (NV, 128), 1)
    r32 = lax.broadcasted_iota(jnp.int32, (NV, 128), 0)
    eye = jnp.where(l32 == r32 + NV, 1.0, 0.0)
    e16r = lax.broadcasted_iota(jnp.int32, (2 * NR, 128), 0)
    e16l = lax.broadcasted_iota(jnp.int32, (2 * NR, 128), 1)
    corrs, mats = [], []
    for s in range(count):
        corr = jnp.concatenate([tile(NV // 8 + b, s * NV) for b in range(2)], 0)[:, :NV]
        corrs.append(corr)
        cor[s] = corr
        a00 = tile(0, base + s * NR)
        a11 = pltpu.roll(tile(0, base + (s + 2) * NR), NR, 1)
        a01 = pltpu.roll(tile(1, base + (s + 2) * NR), NR, 1)
        a10 = tile(2, base + s * NR)
        b = jnp.concatenate([jnp.where(l8 < NR, a00, a01), jnp.where(l8 < NR, a10, a11)], 0)
        b = jnp.where(e16r == e16l, 2.0, 0.0) - b
        b = b[:, :2 * NR]
        bc = lax.dot_general(b, corr, (((1,), (0,)), ((), ())), precision=HP, preferred_element_type=jnp.float32)
        sub = lax.dot_general(corr, bc, (((0,), (0,)), ((), ())), precision=HP, preferred_element_type=jnp.float32)
        ff = jnp.concatenate([tile(b_, s * NV) for b_ in range(NV // 8)], 0)
        sub = jnp.concatenate([sub, jnp.zeros((NV, 128 - NV), jnp.float32)], 1)
        mats.append(jnp.where(l32 < NV, ff - sub, eye)[None])
    M = jnp.concatenate(mats, 0)
    rows = lax.broadcasted_iota(jnp.int32, (1, NV, 1), 1)
    for k in range(NV):
        pivot = M[:, k:k + 1, :]
        inv = 1.0 / pivot[:, :, k:k + 1]
        f = jnp.where(rows > k, M[:, :, k:k + 1] * inv, 0.0)
        M = M - f * pivot
    diag = jnp.sum(jnp.where(l32[None] == r32[None], M, 0.0), axis=2, keepdims=True)
    M = M * (1.0 / jnp.sqrt(diag))
    ident = jnp.where(l32 == r32, 1.0, 0.0)[:, :NV]
    for s in range(count):
        linv = pltpu.roll(M[s], 128 - NV, 1)[:, :NV]
        full = jnp.concatenate([ident, -corrs[s]], 0)
        LM[s] = lax.dot_general(linv, full, contract, precision=HP, preferred_element_type=jnp.float32)

    def finish(s, carry):
        left = LM[s]
        for x in range(X):
            z = [jnp.concatenate([FA[s, x, r], RA[s, x, r], RA[s + 2, x, r]], 0) for r in range(Y)]
            z = jnp.concatenate(z, 1)
            o = lax.dot_general(left, z, (((1,), (0,)), ((), ())), precision=HP, preferred_element_type=jnp.float32)
            for r in range(Y):
                out[s, pl.ds(x * Y + r, NV, stride=J), :] = o[:, r * NZ:(r + 1) * NZ]
        return carry

    lax.fori_loop(0, count, finish, 0)
    for copy in pending:
        copy.wait_send()


def on_device(disorder, slice_bounds, start, ritz):
    nc, nx, ny = (lax.axis_size(a) for a in ("cuts", "lx", "ly"))
    count, NV, X, Y, NZ = start.shape
    NR = ritz.shape[1]
    J = X * Y
    S, R, K, ng = count // 2, 2 * Y, ny // 2, nx * 2
    CH = 1
    NC, W = S * CH, NV // CH
    NL = count * NV + (count + 2) * NR
    tg = -(-((NV + 2 * NR) // 8 * (NL // 128)) // ng)
    f32 = jnp.float32
    V = pltpu.VMEM
    D = pltpu.SemaphoreType.DMA
    dims = (nc, nx, ny, count, NV, NR, X, Y, NZ)
    vm = pl.BlockSpec(memory_space=pltpu.VMEM)
    hbm = pl.BlockSpec(memory_space=pl.ANY)
    block, corr = pl.pallas_call(
        functools.partial(kernel, dims),
        out_shape=(jax.ShapeDtypeStruct((count, NV * J, NZ), f32),
                   jax.ShapeDtypeStruct((count, 2 * NR, NV), f32)),
        in_specs=[hbm, pl.BlockSpec(memory_space=pltpu.SMEM), hbm, hbm],
        out_specs=(vm, vm),
        scratch_shapes=[
            V((J, NZ), jnp.int32),
            V((count, NV * J, NZ), f32),
            V((count, NR * J, NZ), f32),
            D((2 * S + 2,)),
            V((NC, X + 2 * H, R + 2 * H, W, NZ), f32),
            V((NC, X, Y, W, NZ), f32),
            V((X + 2 * H, R + 2 * H, 8, NZ), f32),
            V((X + 2 * H, R + 2 * H, W, NZ), f32),
            V((count, X, Y, NV, NZ), f32),
            V((NC, X, Y, W, NZ), f32),
            V((count + 2, X, Y, NR, NZ), f32),
            V((NL, NL), f32),
            V((count, NV, NV + 2 * NR), f32),
            V((ng * tg, 8, 128), f32),
            V((ng, tg, 8, 128), f32),
            V((K, tg, 8, 128), f32),
            V((tg, 8, 128), f32),
            V((ng, tg, 8, 128), f32),
            D((NC + 1, 9)), D((NC + 1, 9)), D((NC,)), D((NC,)), D((2,)), D((2,)),
            D((ng,)), D((ng,)), D((K,)), D((K,)), D((ng,)), D((ng,)),
        ],
        compiler_params=pltpu.CompilerParams(collective_id=0, has_side_effects=True, vmem_limit_bytes=67043328),
    )(disorder.reshape(J, NZ), slice_bounds.T, start.reshape(count, NV * J, NZ), ritz.reshape(count, NR * J, NZ))
    return (block.reshape(start.shape), corr)


def solution(mesh):
    in_specs = (
        P("lx", "ly", None),
        P("cuts", None),
        P("cuts", None, "lx", "ly", None),
        P("cuts", None, "lx", "ly", None),
    )
    out_specs = (P("cuts", None, "lx", "ly", None), P("cuts", None, None))
    return jax.shard_map(
        on_device, mesh=mesh, in_specs=in_specs, out_specs=out_specs, check_vma=False
    )
```

profile of v0, /device:TPU:0, one launch (start us, length us, event | category | flops | bytes accessed | tf_op | source)
XLA Modules:
  0.0 82.9 jit_solution(12662635849433333346)
XLA Ops:
  0.6 78.5 %shard_map.59 = (f32[6,512,128]{2,1,0:T(8,128)}, f32[6,16,32]{2,1,0:T(8,128)}) custom-call(s32[16,128]{1,0:T(8,128)} %bitcast.8, f32[2,6]{1,0:T(2,128)} %bitcast.9, f32[6,512,128]{2,1,0:T(8,128)} %bitcast.5, f32[6,128,128]{2,1,0:T(8,128)} %bitcast.7), custom_call_target="tpu_custom_call" | custom-call | tf_op jit(solution)/shard_map/pallas_call | solution.py:365
  79.2 0.0 copy-start
  79.2 3.1 %copy.8 = f32[6,32,8,2,128]{4,3,2,1,0:T(2,128)} copy(f32[6,32,8,2,128]{4,3,2,1,0:T(2,128)} %bitcast.6) | data formatting | bytes 3145728
  82.3 0.0 copy-done
  82.3 0.6 copy.9
Async XLA Ops:
  79.2 3.2 %copy-start = (f32[6,16,32]{2,1,0:T(8,128)S(1)}, f32[6,16,32]{2,1,0:T(8,128)}, u32[]{:S(2)}) copy-start(f32[6,16,32]{2,1,0:T(8,128)} %get-tuple-element.9) | copy-start | bytes 36868
where the time goes:
time: 83.1 us; the launch traced here: 82.9 us
  Pallas kernels  78.5 us (94%)
  local copies, waits for them, and re-layouts  3.77 us (5%)
    pallas_call x1, Pallas kernels, on_device(): pl.pallas_call(functools.partial(kernel, dims), out_shape=(jax.ShapeDtype...  78.5 us
    unnamed x4, local copies, waits for them, and re-layouts  3.77 us

commit v1 on v0

v1 whole, which is shorter than its diff:
```python
import functools

import jax
import jax.numpy as jnp
from jax import lax
from jax.experimental import pallas as pl
from jax.experimental.pallas import tpu as pltpu
from jax.sharding import PartitionSpec as P

LEVELS = 256
MESH = pl.DeviceIdType.MESH
HP = lax.Precision.HIGHEST
H = 2
BF = jnp.bfloat16
F32 = jnp.float32
NT = (((1,), (1,)), ((), ()))
NN = (((1,), (0,)), ((), ()))
TN = (((0,), (0,)), ((), ()))


def sem_counts(nx, K, S):
    groups = 2
    one = 4 + S * 13 + 2 + (S + 2) + S
    return one + groups * (nx + K)


def split(z):
    hi = z.astype(BF)
    return hi, (z - hi.astype(F32)).astype(BF)


def kernel(dims, dis_h, bnd, start_h, ritz_h, out, cor, dis, start, ritz, ls, E, T, O, U, FA, FT, RA, RQ,
           PK, RX, SM, RZ, LM, LP, LR, ss, rs):
    nc, nx, ny, count, NV, NR, X, Y, NZ = dims
    S = count // 2
    R = 2 * Y
    J = X * Y
    K = ny // 2
    total = float(J * NZ * nx * ny)
    NW = 2 * NR
    NB = NV + NW
    cut, mx, my = lax.axis_index("cuts"), lax.axis_index("lx"), lax.axis_index("ly")
    p = lax.rem(my, 2)
    q = 1 - p
    kz = my // 2
    yp = (cut, mx, kz * 2 + q)
    zup = (cut, mx, lax.rem(kz + 1, K) * 2 + p)
    zdown = (cut, mx, lax.rem(kz + K - 1, K) * 2 + p)
    xup = (cut, lax.rem(mx + 1, nx), my)
    xdown = (cut, lax.rem(mx + nx - 1, nx), my)
    cup = (lax.rem(cut + 1, nc), mx, my)
    cdown = (lax.rem(cut + nc - 1, nc), mx, my)

    def load(src, dst, i):
        copy = pltpu.make_async_copy(src, dst, ls.at[i])
        copy.start()
        return copy

    level_load = load(dis_h, dis, 2 * S)
    away, kept = [], []
    for c in range(S):
        away.append(load(start_h.at[q * S + c], start.at[c], c))
        kept.append(load(start_h.at[p * S + c], start.at[S + c], S + c))
    ritz_load = load(ritz_h, ritz, 2 * S + 1)
    barrier = pltpu.get_barrier_semaphore()

    def greet(dev):
        pl.semaphore_signal(barrier, inc=1, device_id=dev, device_id_type=MESH)

    greet(yp)
    for o in range(1, nx):
        greet((cut, lax.rem(mx + o, nx), my))
    for o in range(1, K):
        greet((cut, mx, lax.rem(kz + o, K) * 2 + p))
    greet(cup)
    greet(cdown)

    lo = H + Y * p
    lq = H + Y * q
    xi = pl.ds(H, X)
    level_load.wait()
    for x in range(X):
        for r in range(Y):
            row = dis[pl.ds(x * Y + r, 1), :].astype(F32)
            O[H + x, lo + r] = 16.5 * (row / F32(LEVELS - 1) - 0.5)

    def stage_away(c):
        away[c].wait()
        for x in range(X):
            for r in range(Y):
                T[c, x, r] = start[c, pl.ds(x * Y + r, NV, stride=J), :]

    def stage_kept(c):
        kept[c].wait()
        for x in range(X):
            for r in range(Y):
                E[c, H + x, lo + r] = start[S + c, pl.ds(x * Y + r, NV, stride=J), :]

    pending = []
    used = [0]

    def slots(n=1):
        i = used[0]
        used[0] += n
        return i

    def send(src, dst, i, j, dev):
        copy = pltpu.make_async_remote_copy(
            src_ref=src, dst_ref=dst, send_sem=ss.at[i], recv_sem=rs.at[j], device_id=dev, device_id_type=MESH)
        copy.start()
        pending.append(copy)

    def arrived(dst, j):
        pltpu.make_async_remote_copy(
            src_ref=dst, dst_ref=dst, send_sem=rs.at[j], recv_sem=rs.at[j],
            device_id=yp, device_id_type=MESH).wait_recv()

    def rows(at):
        return pl.ds(at, Y)

    o_y, o_z, o_x = slots(), slots(2), slots(2)
    y_at = [slots() for _ in range(S)]
    z_at = [slots(2) for _ in range(S)]
    xo_at = [slots(2) for _ in range(S)]
    xp_at = [slots(2) for _ in range(S)]
    k_at = [slots(4) for _ in range(S)]
    f_at = [slots() for _ in range(S)]
    l_at = [slots() for _ in range(S)]
    c_at = slots(2)
    r_at = slots(S + 2)
    groups = [list(range(S - 1)), [S - 1]]
    ax_at = [slots(nx) for _ in groups]
    az_at = [slots(K) for _ in groups]

    def send_y(c):
        send(T.at[c], E.at[c, xi, rows(lo)], y_at[c], y_at[c], yp)

    def send_z(c, half):
        side = 1 - half
        dev = (cut, mx, jnp.where(half == 1, zup[2], zdown[2]))
        dst = jnp.where(half == 1, 0, H + R)
        send(E.at[c, xi, rows(H + Y * half)], E.at[c, xi, rows(dst)], z_at[c] + side, z_at[c] + side, dev)

    def send_x(c, base, at):
        send(E.at[c, pl.ds(X, H), rows(at)], E.at[c, pl.ds(0, H), rows(at)], base, base, xup)
        send(E.at[c, pl.ds(H, H), rows(at)], E.at[c, pl.ds(H + X, H), rows(at)], base + 1, base + 1, xdown)

    def got_x(c, base, at):
        arrived(E.at[c, pl.ds(0, H), rows(at)], base)
        arrived(E.at[c, pl.ds(H + X, H), rows(at)], base + 1)

    def send_o(half):
        side = 1 - half
        dev = (cut, mx, jnp.where(half == 1, zup[2], zdown[2]))
        src = jnp.where(half == 1, H + R - 1, H)
        dst = jnp.where(half == 1, 1, H + R)
        send(O.at[xi, src], O.at[xi, dst], o_z + side, o_z + side, dev)

    stage_away(0)
    stage_kept(0)
    pl.semaphore_wait(barrier, nx + K + 1)
    send(O.at[xi, rows(lo)], O.at[xi, rows(lo)], o_y, o_y, yp)
    send_y(0)
    send_o(p)
    send_z(0, p)
    send_x(0, xo_at[0], lo)
    for c in range(1, S):
        stage_away(c)
        send_y(c)
        stage_kept(c)
        if c < S - 1:
            send_z(c, p)
        send_x(c, xo_at[c], lo)
    ritz_load.wait()
    for s in range(count):
        for x in range(X):
            for r in range(Y):
                RA[s + 1, x, r] = ritz[s, pl.ds(x * Y + r, NR, stride=J), :]
    send(RA.at[count], RA.at[0], c_at, c_at, cup)
    send(RA.at[1], RA.at[count + 1], c_at + 1, c_at + 1, cdown)

    own = pl.ds(H, R)
    arrived(O.at[xi, rows(lq)], o_y)
    send_o(q)
    send(O.at[H + X - 1, own], O.at[H - 1, own], o_x, o_x, xup)
    send(O.at[H, own], O.at[H + X, own], o_x + 1, o_x + 1, xdown)

    arrived(RA.at[0], c_at)
    arrived(RA.at[count + 1], c_at + 1)

    @pl.when(cut == 0)
    def _():
        RA[0] = jnp.zeros((X, Y, NR, NZ), F32)

    @pl.when(cut == nc - 1)
    def _():
        RA[count + 1] = jnp.zeros((X, Y, NR, NZ), F32)

    order = []
    for c in range(S):
        for j in (c, c + 2):
            if j not in order:
                order.append(j)
    for j in order:
        send(RA.at[q * S + j], RQ.at[j], r_at + j, r_at + j, yp)

    for c in range(S):
        arrived(E.at[c, xi, rows(lq)], y_at[c])
        send_z(c, q)
        send_x(c, xp_at[c], lq)
        if c == 0:
            send_z(S - 1, p)

    arrived(O.at[xi, H - 1], o_z)
    arrived(O.at[xi, H + R], o_z + 1)
    arrived(O.at[H - 1, own], o_x)
    arrived(O.at[H + X, own], o_x + 1)

    def point(src, x, r, centre):
        v = src(x, r)
        beside = src(x + 1, r) + src(x - 1, r)
        beside = beside + src(x, r + 1) + src(x, r - 1)
        beside = beside + pltpu.roll(v, 1, 1) + pltpu.roll(v, NZ - 1, 1)
        level = jnp.broadcast_to(O[x, r] - centre, (NV, NZ))
        return (level * v - beside) * 0.0625

    def apply(c):
        s = p * S + c
        centre = (bnd[0, s] + bnd[1, s]) / 2.0
        got_x(c, xo_at[c], lo)
        got_x(c, xp_at[c], lq)
        for early in (1, 0):
            side = q if early else p
            row = jnp.where(side == 1, H + R, H - 1)
            arrived(E.at[c, xi, rows(jnp.where(side == 1, H + R, 0))], z_at[c] + side)
            k = k_at[c] + 2 * side
            send(E.at[c, H + X - 1, row], E.at[c, H - 1, row], k, k, xup)
            send(E.at[c, H, row], E.at[c, H + X, row], k + 1, k + 1, xdown)

        def from_e(x, r):
            return E[c, x, r]

        def from_u(x, r):
            return U[x, r]

        def first(i, carry):
            for r in range(H - 1, H + R + 1):
                U[H + 1 + i, r] = point(from_e, H + 1 + i, r, centre)
            return carry

        lax.fori_loop(0, X - 2, first, 0)
        for x in (H, H + X - 1):
            for r in range(H, H + R):
                U[x, r] = point(from_e, x, r, centre)
        for x in (H - 1, H + X):
            for r in range(H + 1, H + R - 1):
                U[x, r] = point(from_e, x, r, centre)
        for side, row in ((0, H - 1), (1, H + R)):
            arrived(E.at[c, H - 1, row], k_at[c] + 2 * side)
            arrived(E.at[c, H + X, row], k_at[c] + 2 * side + 1)
        for x in (H, H + X - 1):
            for r in (H - 1, H + R):
                U[x, r] = point(from_e, x, r, centre)
        for x in (H - 1, H + X):
            for r in (H, H + R - 1):
                U[x, r] = point(from_e, x, r, centre)

        def second(i, carry):
            for r in range(Y):
                FT[c, i, r] = 2.0 * point(from_u, H + i, lq + r, centre) - E[c, H + i, lq + r]
                FA[s, i, r] = 2.0 * point(from_u, H + i, lo + r, centre) - E[c, H + i, lo + r]
            return carry

        lax.fori_loop(0, X, second, 0)
        send(FT.at[c], FA.at[s], f_at[c], f_at[c], yp)

    def gram(c):
        s = p * S + c
        arrived(RQ.at[c], r_at + c) if c < 2 else None
        arrived(RQ.at[c + 2], r_at + c + 2)

        def body(i, carry):
            a, b = carry
            for k in range(2):
                if k == 0:
                    z = [jnp.concatenate([FA[s, i, r], RA[s, i, r], RA[s + 2, i, r]], 0) for r in range(Y)]
                else:
                    z = [jnp.concatenate([FT[c, i, r], RQ[c, i, r], RQ[c + 2, i, r]], 0) for r in range(Y)]
                hi, lw = split(jnp.concatenate(z, 1))
                both = jnp.concatenate([hi, lw], 0)
                a = a + lax.dot_general(both, hi, NT, preferred_element_type=F32)
                b = b + lax.dot_general(both, lw, NT, preferred_element_type=F32)
            return a, b

        zero = jnp.zeros((2 * NB, NB), F32)
        a, b = lax.fori_loop(0, X, body, (zero, zero))
        g = (a[:NB] + b[NB:]) + (a[NB:] + b[:NB])
        g = jnp.concatenate([g, jnp.zeros((NB, 128 - NB), F32)], 1)
        lane = lax.broadcasted_iota(jnp.int32, (8, 128), 1)
        t0 = jnp.zeros((8, 128), F32)
        for b_ in range(NV // 8):
            piece = jnp.where(lane < NV, g[b_ * 8:b_ * 8 + 8], 0.0)
            t0 = t0 + (pltpu.roll(piece, b_ * NV, 1) if b_ else piece)
        t1 = g[NV:NV + 8] + pltpu.roll(g[NV + 8:NV + 16], 64, 1)
        PK[c, 0] = t0
        PK[c, 1] = t1

    def sum_x_start(k):
        cs = groups[k]
        part = pl.ds(cs[0], len(cs))
        for c in cs:
            RX[mx, c] = PK[c]
        for o in range(1, nx):
            send(PK.at[part], RX.at[mx, part], ax_at[k] + o, ax_at[k] + mx, (cut, lax.rem(mx + o, nx), my))

    def sum_x_end(k):
        cs = groups[k]
        part = pl.ds(cs[0], len(cs))
        for o in range(1, nx):
            t = lax.rem(mx + o, nx)
            arrived(RX.at[t, part], ax_at[k] + t)
        for c in cs:
            acc = RX[0, c]
            for t in range(1, nx):
                acc = acc + RX[t, c]
            SM[c] = acc
            RZ[kz, c] = acc
        for o in range(1, K):
            t = lax.rem(kz + o, K)
            send(SM.at[part], RZ.at[kz, part], az_at[k] + o, az_at[k] + kz, (cut, mx, t * 2 + p))

    e16r = lax.broadcasted_iota(jnp.int32, (NW, NW), 0)
    e16l = lax.broadcasted_iota(jnp.int32, (NW, NW), 1)
    l32 = lax.broadcasted_iota(jnp.int32, (NV, 128), 1)
    r32 = lax.broadcasted_iota(jnp.int32, (NV, 128), 0)
    eye = jnp.where(l32 == r32 + NV, 1.0, 0.0)
    ident = jnp.where(l32 == r32, 1.0, 0.0)[:, :NV]

    def factor(k):
        cs = groups[k]
        part = pl.ds(cs[0], len(cs))
        for o in range(1, K):
            t = lax.rem(kz + o, K)
            arrived(RZ.at[t, part], az_at[k] + t)
        corrs, mats = [], []
        for c in cs:
            acc = RZ[0, c]
            for t in range(1, K):
                acc = acc + RZ[t, c]
            acc = acc * (1.0 / total)
            t0, t1 = acc[0], acc[1]
            ff = jnp.concatenate([pltpu.roll(t0, 128 - b * NV, 1) if b else t0 for b in range(NV // 8)], 0)
            w = jnp.concatenate([t1, pltpu.roll(t1, 64, 1)], 0)
            corr = w[:, :NV]
            b = jnp.where(e16r == e16l, 2.0, 0.0) - pltpu.roll(w, 128 - NV, 1)[:, :NW]
            bc = lax.dot_general(b, corr, NN, precision=HP, preferred_element_type=F32)
            sub = lax.dot_general(corr, bc, TN, precision=HP, preferred_element_type=F32)
            sub = jnp.concatenate([sub, jnp.zeros((NV, 128 - NV), F32)], 1)
            corrs.append(corr)
            mats.append(jnp.where(l32 < NV, ff - sub, eye)[None])
        M = jnp.concatenate(mats, 0)
        line = lax.broadcasted_iota(jnp.int32, (1, NV, 1), 1)
        for j in range(NV):
            pivot = M[:, j:j + 1, :]
            inv = 1.0 / pivot[:, :, j:j + 1]
            f = jnp.where(line > j, M[:, :, j:j + 1] * inv, 0.0)
            M = M - f * pivot
        diag = jnp.sum(jnp.where(l32[None] == r32[None], M, 0.0), axis=2, keepdims=True)
        M = M * (1.0 / jnp.sqrt(diag))
        for i, c in enumerate(cs):
            s = p * S + c
            linv = pltpu.roll(M[i], 128 - NV, 1)[:, :NV]
            full = jnp.concatenate([ident, -corrs[i]], 0)
            lm = lax.dot_general(linv, full, NT, precision=HP, preferred_element_type=F32)
            LM[s] = lm
            cor[s] = corrs[i]
            wide = jnp.concatenate([corrs[i], jnp.zeros((NV - NW, NV), F32)], 0)
            wide = jnp.concatenate([lm, jnp.zeros((NV, 64 - NB), F32), wide, jnp.zeros((NV, 64 - NV), F32)], 1)
            LP[c] = wide
            send(LP.at[c], LR.at[c], l_at[c], l_at[c], yp)

    def take(c):
        s = q * S + c
        arrived(LR.at[c], l_at[c])
        wide = LR[c]
        LM[s] = wide[:, :NB]
        cor[s] = pltpu.roll(wide, 64, 1)[:NW, :NV]
        arrived(FA.at[s], f_at[c])

    def finish(s):
        hi, lw = split(LM[s])
        left = jnp.concatenate([hi, hi, lw], 1)

        def body(x, carry):
            z = [jnp.concatenate([FA[s, x, r], RA[s, x, r], RA[s + 2, x, r]], 0) for r in range(Y)]
            zh, zl = split(jnp.concatenate(z, 1))
            o = lax.dot_general(left, jnp.concatenate([zh, zl, zh], 0), NN, preferred_element_type=F32)
            for r in range(Y):
                out[s, pl.ds(x * Y + r, NV, stride=J), :] = o[:, r * NZ:(r + 1) * NZ]
            return carry

        lax.fori_loop(0, X, body, 0)

    for c in range(S - 1):
        apply(c)
        gram(c)
    sum_x_start(0)
    sum_x_end(0)
    apply(S - 1)
    gram(S - 1)
    sum_x_start(1)
    sum_x_end(1)
    factor(0)
    for c in groups[0]:
        finish(p * S + c)
    factor(1)
    for c in groups[0]:
        take(c)
        finish(q * S + c)
    finish(p * S + S - 1)
    take(S - 1)
    finish(q * S + S - 1)
    for copy in pending:
        copy.wait_send()


def on_device(disorder, slice_bounds, start, ritz):
    nc, nx, ny = (lax.axis_size(a) for a in ("cuts", "lx", "ly"))
    count, NV, X, Y, NZ = start.shape
    NR = ritz.shape[1]
    J = X * Y
    S, R, K = count // 2, 2 * Y, ny // 2
    V = pltpu.VMEM
    D = pltpu.SemaphoreType.DMA
    dims = (nc, nx, ny, count, NV, NR, X, Y, NZ)
    vm = pl.BlockSpec(memory_space=pltpu.VMEM)
    hbm = pl.BlockSpec(memory_space=pl.ANY)
    sems = sem_counts(nx, K, S)
    block, corr = pl.pallas_call(
        functools.partial(kernel, dims),
        out_shape=(jax.ShapeDtypeStruct((count, NV * J, NZ), F32),
                   jax.ShapeDtypeStruct((count, 2 * NR, NV), F32)),
        in_specs=[hbm, pl.BlockSpec(memory_space=pltpu.SMEM), hbm, hbm],
        out_specs=(vm, vm),
        scratch_shapes=[
            V((J, NZ), jnp.int32),
            V((count, NV * J, NZ), F32),
            V((count, NR * J, NZ), F32),
            D((2 * S + 2,)),
            V((S, X + 2 * H, R + 2 * H, NV, NZ), F32),
            V((S, X, Y, NV, NZ), F32),
            V((X + 2 * H, R + 2 * H, 1, NZ), F32),
            V((X + 2 * H, R + 2 * H, NV, NZ), F32),
            V((count, X, Y, NV, NZ), F32),
            V((S, X, Y, NV, NZ), F32),
            V((count + 2, X, Y, NR, NZ), F32),
            V((S + 2, X, Y, NR, NZ), F32),
            V((S, 2, 8, 128), F32),
            V((nx, S, 2, 8, 128), F32),
            V((S, 2, 8, 128), F32),
            V((K, S, 2, 8, 128), F32),
            V((count, NV, NV + 2 * NR), F32),
            V((S, NV, 128), F32),
            V((S, NV, 128), F32),
            D((sems,)), D((sems,)),
        ],
        compiler_params=pltpu.CompilerParams(collective_id=0, has_side_effects=True, vmem_limit_bytes=67043328),
    )(disorder.reshape(J, NZ), slice_bounds.T, start.reshape(count, NV * J, NZ), ritz.reshape(count, NR * J, NZ))
    return (block.reshape(start.shape), corr)


def solution(mesh):
    in_specs = (
        P("lx", "ly", None),
        P("cuts", None),
        P("cuts", None, "lx", "ly", None),
        P("cuts", None, "lx", "ly", None),
    )
    out_specs = (P("cuts", None, "lx", "ly", None), P("cuts", None, None))
    return jax.shard_map(
        on_device, mesh=mesh, in_specs=in_specs, out_specs=out_specs, check_vma=False
    )
```

time: 83.1 us -> 75.3 us (0.906)
  Pallas kernels: 78.5 us -> 70.7 us
    pallas_call x1, Pallas kernels: 78.5 us -> 70.7 us  [on_device(): pl.pallas_call(functools.partial(kernel, dims), out_shape=(jax.ShapeDtype...]
where the time goes in v1:
time: 75.3 us; the launch traced here: 75.1 us
  Pallas kernels  70.7 us (94%)
  local copies, waits for them, and re-layouts  3.77 us (5%)
    pallas_call x1, Pallas kernels, on_device(): pl.pallas_call(functools.partial(kernel, dims), out_shape=(jax.ShapeDtype...  70.7 us
    unnamed x4, local copies, waits for them, and re-layouts  3.77 us

profile of v1, /device:TPU:0, one launch (start us, length us, event | category | flops | bytes accessed | tf_op | source)
XLA Modules:
  0.0 75.1 jit_solution(5053960559587867570)
XLA Ops:
  0.6 70.7 %shard_map.59 = (f32[6,512,128]{2,1,0:T(8,128)}, f32[6,16,32]{2,1,0:T(8,128)}) custom-call(s32[16,128]{1,0:T(8,128)} %bitcast.8, f32[2,6]{1,0:T(2,128)} %bitcast.9, f32[6,512,128]{2,1,0:T(8,128)} %bitcast.5, f32[6,128,128]{2,1,0:T(8,128)} %bitcast.7), custom_call_target="tpu_custom_call" | custom-call | tf_op jit(solution)/shard_map/pallas_call | solution.py:439
  71.3 0.0 copy-start
  71.3 3.1 %copy.8 = f32[6,32,8,2,128]{4,3,2,1,0:T(2,128)} copy(f32[6,32,8,2,128]{4,3,2,1,0:T(2,128)} %bitcast.6) | data formatting | bytes 3145728
  74.5 0.0 copy-done
  74.5 0.6 copy.9
Async XLA Ops:
  71.3 3.2 %copy-start = (f32[6,16,32]{2,1,0:T(8,128)S(1)}, f32[6,16,32]{2,1,0:T(8,128)}, u32[]{:S(2)}) copy-start(f32[6,16,32]{2,1,0:T(8,128)} %get-tuple-element.9) | copy-start | bytes 36868

commit v2 on v1

v2 whole, which is shorter than its diff:
```python
import functools

import jax
import jax.numpy as jnp
from jax import lax
from jax.experimental import pallas as pl
from jax.experimental.pallas import tpu as pltpu
from jax.sharding import PartitionSpec as P

LEVELS = 256
MESH = pl.DeviceIdType.MESH
HP = lax.Precision.HIGHEST
H = 2
BF = jnp.bfloat16
F32 = jnp.float32
NT = (((1,), (1,)), ((), ()))
NN = (((1,), (0,)), ((), ()))
TN = (((0,), (0,)), ((), ()))


def sem_counts(nx, K, S):
    return 5 + S * (14 + nx + K) + 2 + (S + 2)


def split(z):
    hi = z.astype(BF)
    return hi, (z - hi.astype(F32)).astype(BF)


def loop(n, unroll, body):
    def step(i, carry):
        for k in range(unroll):
            body(i * unroll + k)
        return carry

    if n % unroll:
        unroll = 1
    lax.fori_loop(0, n // unroll, step, 0)


def kernel(dims, dis_h, bnd_h, start_h, ritz_h, out_h, cor_h, out, cor, bnd, dis, start, ritz, ls, E, T, O, U, FA, FT,
           RA, RQ, GS, PK, RX, SM, RZ, LM, LP, LR, ss, rs):
    nc, nx, ny, count, NV, NR, X, Y, NZ = dims
    S = count // 2
    R = 2 * Y
    J = X * Y
    K = ny // 2
    total = float(J * NZ * nx * ny)
    NW = 2 * NR
    NB = NV + NW
    cut, mx, my = lax.axis_index("cuts"), lax.axis_index("lx"), lax.axis_index("ly")
    p = lax.rem(my, 2)
    q = 1 - p
    kz = my // 2
    yp = (cut, mx, kz * 2 + q)
    zup = (cut, mx, lax.rem(kz + 1, K) * 2 + p)
    zdown = (cut, mx, lax.rem(kz + K - 1, K) * 2 + p)
    xup = (cut, lax.rem(mx + 1, nx), my)
    xdown = (cut, lax.rem(mx + nx - 1, nx), my)
    cup = (lax.rem(cut + 1, nc), mx, my)
    cdown = (lax.rem(cut + nc - 1, nc), mx, my)

    def load(src, dst, i):
        copy = pltpu.make_async_copy(src, dst, ls.at[i])
        copy.start()
        return copy

    level_load = load(dis_h, dis, 2 * S)
    bound_load = load(bnd_h, bnd, 2 * S + 2)
    away, kept = [], []
    for c in range(S):
        away.append(load(start_h.at[q * S + c], start.at[c], c))
        kept.append(load(start_h.at[p * S + c], start.at[S + c], S + c))
    ritz_load = load(ritz_h, ritz, 2 * S + 1)
    barrier = pltpu.get_barrier_semaphore()

    def greet(dev):
        pl.semaphore_signal(barrier, inc=1, device_id=dev, device_id_type=MESH)

    greet(yp)
    for o in range(1, nx):
        greet((cut, lax.rem(mx + o, nx), my))
    for o in range(1, K):
        greet((cut, mx, lax.rem(kz + o, K) * 2 + p))
    greet(cup)
    greet(cdown)

    lo = H + Y * p
    lq = H + Y * q
    xi = pl.ds(H, X)
    level_load.wait()
    for x in range(X):
        for r in range(Y):
            row = dis[pl.ds(x * Y + r, 1), :].astype(F32)
            O[H + x, lo + r] = 16.5 * (row / F32(LEVELS - 1) - 0.5)

    def stage_away(c):
        away[c].wait()
        for x in range(X):
            for r in range(Y):
                T[c, x, r] = start[c, pl.ds(x * Y + r, NV, stride=J), :]

    def stage_kept(c):
        kept[c].wait()
        for x in range(X):
            for r in range(Y):
                E[c, H + x, lo + r] = start[S + c, pl.ds(x * Y + r, NV, stride=J), :]

    pending = []
    used = [0]

    def slots(n=1):
        i = used[0]
        used[0] += n
        return i

    def send(src, dst, i, j, dev):
        copy = pltpu.make_async_remote_copy(
            src_ref=src, dst_ref=dst, send_sem=ss.at[i], recv_sem=rs.at[j], device_id=dev, device_id_type=MESH)
        copy.start()
        pending.append(copy)

    def arrived(dst, j):
        pltpu.make_async_remote_copy(
            src_ref=dst, dst_ref=dst, send_sem=rs.at[j], recv_sem=rs.at[j],
            device_id=yp, device_id_type=MESH).wait_recv()

    def rows(at):
        return pl.ds(at, Y)

    o_y, o_z, o_x = slots(), slots(2), slots(2)
    y_at = [slots() for _ in range(S)]
    z_at = [slots(3) for _ in range(S)]
    xo_at = [slots(2) for _ in range(S)]
    xp_at = [slots(2) for _ in range(S)]
    k_at = [slots(4) for _ in range(S)]
    f_at = [slots() for _ in range(S)]
    l_at = [slots() for _ in range(S)]
    c_at = slots(2)
    r_at = slots(S + 2)
    ax_at = [slots(nx) for _ in range(S)]
    az_at = [slots(K) for _ in range(S)]

    def send_y(c):
        send(T.at[c], E.at[c, xi, rows(lo)], y_at[c], y_at[c], yp)

    def send_own_z(c):
        dev = (cut, mx, jnp.where(p == 1, zup[2], zdown[2]))
        dst = jnp.where(p == 1, 0, H + R)
        send(E.at[c, xi, rows(lo)], E.at[c, xi, rows(dst)], z_at[c], z_at[c], dev)

    def send_rest_z(c):
        dev = (cut, mx, jnp.where(q == 1, zup[2], zdown[2]))
        for k in range(2):
            src = jnp.where(q == 1, H + R - 1 - k, H + k)
            dst = jnp.where(q == 1, H - 1 - k, H + R + k)
            send(E.at[c, xi, src], E.at[c, xi, dst], z_at[c] + 1 + k, z_at[c] + 1 + k, dev)

    def send_x(c, base, at):
        send(E.at[c, pl.ds(X, H), rows(at)], E.at[c, pl.ds(0, H), rows(at)], base, base, xup)
        send(E.at[c, pl.ds(H, H), rows(at)], E.at[c, pl.ds(H + X, H), rows(at)], base + 1, base + 1, xdown)

    def got_x(c, base, at):
        arrived(E.at[c, pl.ds(0, H), rows(at)], base)
        arrived(E.at[c, pl.ds(H + X, H), rows(at)], base + 1)

    def send_o(half):
        side = 1 - half
        dev = (cut, mx, jnp.where(half == 1, zup[2], zdown[2]))
        src = jnp.where(half == 1, H + R - 1, H)
        dst = jnp.where(half == 1, 1, H + R)
        send(O.at[xi, src], O.at[xi, dst], o_z + side, o_z + side, dev)

    stage_away(0)
    stage_kept(0)
    pl.semaphore_wait(barrier, nx + K + 1)
    send(O.at[xi, rows(lo)], O.at[xi, rows(lo)], o_y, o_y, yp)
    send_y(0)
    send_o(p)
    send_own_z(0)
    send_x(0, xo_at[0], lo)
    for c in range(1, S):
        stage_away(c)
        send_y(c)
        stage_kept(c)
        if c < S - 1:
            send_own_z(c)
        send_x(c, xo_at[c], lo)
    bound_load.wait()
    ritz_load.wait()
    for s in range(count):
        for x in range(X):
            for r in range(Y):
                RA[s + 1, x, r] = ritz[s, pl.ds(x * Y + r, NR, stride=J), :]
    send(RA.at[count], RA.at[0], c_at, c_at, cup)
    send(RA.at[1], RA.at[count + 1], c_at + 1, c_at + 1, cdown)

    own = pl.ds(H, R)
    arrived(O.at[xi, rows(lq)], o_y)
    send_o(q)
    send(O.at[H + X - 1, own], O.at[H - 1, own], o_x, o_x, xup)
    send(O.at[H, own], O.at[H + X, own], o_x + 1, o_x + 1, xdown)

    arrived(RA.at[0], c_at)
    arrived(RA.at[count + 1], c_at + 1)

    @pl.when(cut == 0)
    def _():
        RA[0] = jnp.zeros((X, Y, NR, NZ), F32)

    @pl.when(cut == nc - 1)
    def _():
        RA[count + 1] = jnp.zeros((X, Y, NR, NZ), F32)

    order = []
    for c in range(S):
        for j in (c, c + 2):
            if j not in order:
                order.append(j)
    for j in order:
        send(RA.at[q * S + j], RQ.at[j], r_at + j, r_at + j, yp)

    for c in range(S):
        arrived(E.at[c, xi, rows(lq)], y_at[c])
        if c < S - 1:
            send_rest_z(c)
        send_x(c, xp_at[c], lq)
        if c == 0:
            send_own_z(S - 1)

    arrived(O.at[xi, H - 1], o_z)
    arrived(O.at[xi, H + R], o_z + 1)
    arrived(O.at[H - 1, own], o_x)
    arrived(O.at[H + X, own], o_x + 1)

    last = R + 2 * H - 1
    ra = [a + p * (last - 2 * a) for a in range(last + 1)]
    near, far = H - 1, H + R

    def point(src, x, a, centre):
        v = src(x, a)
        beside = src(x + 1, a) + src(x - 1, a)
        beside = beside + src(x, a + 1) + src(x, a - 1)
        beside = beside + pltpu.roll(v, 1, 1) + pltpu.roll(v, NZ - 1, 1)
        level = jnp.broadcast_to(O[x, ra[a]] - centre, (NV, NZ))
        return level * v - beside

    def refs(c):
        s = p * S + c
        centre = (bnd[0, s] + bnd[1, s]) / 2.0

        def from_e(x, a):
            return E[c, x, ra[a]]

        def from_u(x, a):
            return U[c, x, ra[a]]

        def one(x, a):
            U[c, x, ra[a]] = point(from_e, x, a, centre)

        def two(x, a):
            return point(from_u, x, a, centre) * (2.0 / 256.0) - from_e(x, a)

        return one, two

    def corners(c, a, k):
        send(E.at[c, H + X - 1, ra[a]], E.at[c, H - 1, ra[a]], k, k, xup)
        send(E.at[c, H, ra[a]], E.at[c, H + X, ra[a]], k + 1, k + 1, xdown)

    def got_corners(c, a, k):
        arrived(E.at[c, H - 1, ra[a]], k)
        arrived(E.at[c, H + X, ra[a]], k + 1)

    def early_corners(c):
        arrived(E.at[c, xi, rows(jnp.where(p == 1, 0, H + R))], z_at[c])
        corners(c, far, k_at[c])

    def early(c):
        one, two = refs(c)
        got_x(c, xo_at[c], lo)
        got_x(c, xp_at[c], lq)

        def inner(i):
            for a in range(H + 1, far + 1):
                one(H + 1 + i, a)

        loop(X - 2, 2, inner)
        for x in (H, H + X - 1):
            for a in range(H + 1, far):
                one(x, a)
        for x in (H - 1, H + X):
            for a in range(H + 1, far - 1):
                one(x, a)
        got_corners(c, far, k_at[c])
        for x in (H, H + X - 1):
            one(x, far)
        for x in (H - 1, H + X):
            one(x, far - 1)

        def outer(i):
            for a in range(H + Y, far):
                FT[c, i, ra[a] - lq] = two(H + i, a)

        loop(X, 2, outer)
        send(FT.at[c], FA.at[p * S + c], f_at[c], f_at[c], yp)

    def late(c):
        one, two = refs(c)
        arrived(E.at[c, xi, ra[near]], z_at[c] + 1)
        corners(c, near, k_at[c] + 2)
        arrived(E.at[c, xi, ra[near - 1]], z_at[c] + 2)

        def inner(i):
            for a in (near, H):
                one(H + 1 + i, a)

        loop(X - 2, 2, inner)
        for x in (H, H + X - 1):
            one(x, H)
        got_corners(c, near, k_at[c] + 2)
        for x in (H, H + X - 1):
            one(x, near)
        for x in (H - 1, H + X):
            one(x, H)

        def outer(i):
            for a in range(H, H + Y):
                FA[p * S + c, i, ra[a] - lo] = two(H + i, a)

        loop(X, 2, outer)

    def product(f, w0, w1):
        def body(i, acc):
            for k in range(2):
                z = [jnp.concatenate([f(2 * i + k, r), w0(2 * i + k, r), w1(2 * i + k, r)], 0) for r in range(Y)]
                hi, lw = split(jnp.concatenate(z, 1))
                acc = acc + lax.dot_general(jnp.concatenate([hi, lw], 0), hi, NT, preferred_element_type=F32)
            return acc

        return lax.fori_loop(0, X // 2, body, jnp.zeros((2 * NB, NB), F32))

    def gram_rest(c):
        for j in (c, c + 2):
            if j not in seen:
                arrived(RQ.at[j], r_at + j)
                seen.add(j)
        GS[c] = product(lambda x, r: FT[c, x, r], lambda x, r: RQ[c, x, r], lambda x, r: RQ[c + 2, x, r])

    def gram_own(c):
        s = p * S + c
        g = GS[c] + product(lambda x, r: FA[s, x, r], lambda x, r: RA[s, x, r], lambda x, r: RA[s + 2, x, r])
        g = jnp.concatenate([g, jnp.zeros((2 * NB, 128 - NB), F32)], 1)
        cross = jnp.concatenate([g[NB:], jnp.zeros((128 - NB, 128), F32)], 0)
        g = g[:NB] + (cross + cross.T)[:NB]
        lane = lax.broadcasted_iota(jnp.int32, (8, 128), 1)
        t0 = jnp.zeros((8, 128), F32)
        for b_ in range(NV // 8):
            piece = jnp.where(lane < NV, g[b_ * 8:b_ * 8 + 8], 0.0)
            t0 = t0 + (pltpu.roll(piece, b_ * NV, 1) if b_ else piece)
        t1 = g[NV:NV + 8] + pltpu.roll(g[NV + 8:NV + 16], 64, 1)
        PK[c, 0] = t0
        PK[c, 1] = t1

    seen = set()

    def sum_x_start(c):
        RX[mx, c] = PK[c]
        for o in range(1, nx):
            send(PK.at[c], RX.at[mx, c], ax_at[c] + o, ax_at[c] + mx, (cut, lax.rem(mx + o, nx), my))

    def sum_x_end(c):
        for o in range(1, nx):
            t = lax.rem(mx + o, nx)
            arrived(RX.at[t, c], ax_at[c] + t)
        acc = RX[0, c]
        for t in range(1, nx):
            acc = acc + RX[t, c]
        SM[c] = acc
        RZ[kz, c] = acc
        for o in range(1, K):
            t = lax.rem(kz + o, K)
            send(SM.at[c], RZ.at[kz, c], az_at[c] + o, az_at[c] + kz, (cut, mx, t * 2 + p))

    e16r = lax.broadcasted_iota(jnp.int32, (NW, NW), 0)
    e16l = lax.broadcasted_iota(jnp.int32, (NW, NW), 1)
    l32 = lax.broadcasted_iota(jnp.int32, (NV, 128), 1)
    r32 = lax.broadcasted_iota(jnp.int32, (NV, 128), 0)
    eye = jnp.where(l32 == r32 + NV, 1.0, 0.0)
    ident = jnp.where(l32 == r32, 1.0, 0.0)[:, :NV]

    def factor(c):
        for o in range(1, K):
            t = lax.rem(kz + o, K)
            arrived(RZ.at[t, c], az_at[c] + t)
        acc = RZ[0, c]
        for t in range(1, K):
            acc = acc + RZ[t, c]
        acc = acc * (1.0 / total)
        t0, t1 = acc[0], acc[1]
        ff = jnp.concatenate([pltpu.roll(t0, 128 - b * NV, 1) if b else t0 for b in range(NV // 8)], 0)
        w = jnp.concatenate([t1, pltpu.roll(t1, 64, 1)], 0)
        corr = w[:, :NV]
        b = jnp.where(e16r == e16l, 2.0, 0.0) - pltpu.roll(w, 128 - NV, 1)[:, :NW]
        bc = lax.dot_general(b, corr, NN, precision=HP, preferred_element_type=F32)
        sub = lax.dot_general(corr, bc, TN, precision=HP, preferred_element_type=F32)
        sub = jnp.concatenate([sub, jnp.zeros((NV, 128 - NV), F32)], 1)
        M = jnp.where(l32 < NV, ff - sub, eye)
        line = lax.broadcasted_iota(jnp.int32, (NV, 1), 0)
        for j in range(0, NV, 2):
            r0, r1 = M[j:j + 1], M[j + 1:j + 2]
            c0, c1 = M[:, j:j + 1], M[:, j + 1:j + 2]
            p00, p01, p11 = c0[j:j + 1], c1[j:j + 1], c1[j + 1:j + 2]
            inv = 1.0 / (p00 * p11 - p01 * p01)
            keep = jnp.where(line > j + 1, inv, 0.0)
            f0 = (c0 * p11 - c1 * p01) * keep
            f1 = (c1 * p00 - c0 * p01) * keep
            M = M - f0 * r0 - f1 * r1
        odd = r32 % 2
        diag = jnp.sum(jnp.where(l32 == r32, M, 0.0), axis=1, keepdims=True)
        side = jnp.sum(jnp.where(l32 == r32 - odd, M, 0.0), axis=1, keepdims=True)
        above = pltpu.roll(M, 1, 0)
        ratio = side / pltpu.roll(jnp.broadcast_to(diag, (NV, 128)), 1, 0)
        M = jnp.where(odd == 1, M - ratio * above, M)
        diag = jnp.sum(jnp.where(l32 == r32, M, 0.0), axis=1, keepdims=True)
        M = M * (1.0 / jnp.sqrt(diag))
        s = p * S + c
        linv = pltpu.roll(M, 128 - NV, 1)[:, :NV]
        full = jnp.concatenate([ident, -corr], 0)
        lm = lax.dot_general(linv, full, NT, precision=HP, preferred_element_type=F32)
        wide = jnp.concatenate([corr, jnp.zeros((NV - NW, NV), F32)], 0)
        wide = jnp.concatenate([lm, jnp.zeros((NV, 64 - NB), F32), wide, jnp.zeros((NV, 64 - NV), F32)], 1)
        LP[c] = wide
        send(LP.at[c], LR.at[c], l_at[c], l_at[c], yp)
        LM[s] = lm
        cor[s] = corr

    def take(c):
        s = q * S + c
        arrived(LR.at[c], l_at[c])
        wide = LR[c]
        LM[s] = wide[:, :NB]
        cor[s] = pltpu.roll(wide, 64, 1)[:NW, :NV]
        arrived(FA.at[s], f_at[c])

    stored = []

    def store(src, dst, i):
        stored.append(load(src, dst, i))

    def finish(s, i):
        hi, lw = split(LM[s])
        left = jnp.concatenate([hi, lw], 0)
        left = jnp.concatenate([left, jnp.concatenate([hi, jnp.zeros((NV, NB), BF)], 0)], 1)

        def body(x):
            z = [jnp.concatenate([FA[s, x, r], RA[s, x, r], RA[s + 2, x, r]], 0) for r in range(Y)]
            zh, zl = split(jnp.concatenate(z, 1))
            o = lax.dot_general(left, jnp.concatenate([zh, zl], 0), NN, preferred_element_type=F32)
            o = o[:NV] + o[NV:]
            for r in range(Y):
                out[s, pl.ds(x * Y + r, NV, stride=J), :] = o[:, r * NZ:(r + 1) * NZ]

        loop(X, 2, body)
        store(out.at[s], out_h.at[s], i)

    def finish_own(c):
        finish(p * S + c, c)

    def finish_rest(c):
        take(c)
        finish(q * S + c, S + c)

    early_corners(0)
    early(0)
    late(0)
    gram_rest(0)
    gram_own(0)
    sum_x_start(0)
    for c in range(1, S):
        early_corners(c) if c < S - 1 else None
    for c in range(1, S):
        if c == S - 1:
            sum_x_end(0)
            send_rest_z(c)
            early_corners(c)
        early(c)
        gram_rest(c)
    for c in range(1, S - 1):
        late(c)
        gram_own(c)
        sum_x_start(c)
        factor(c - 1)
        finish_own(c - 1)
        sum_x_end(c)
        finish_rest(c - 1)
    late(S - 1)
    gram_own(S - 1)
    sum_x_start(S - 1)
    sum_x_end(S - 1)
    factor(S - 2)
    finish_own(S - 2)
    factor(S - 1)
    finish_rest(S - 2)
    finish_own(S - 1)
    take(S - 1)
    store(cor, cor_h, 2 * S)
    finish(q * S + S - 1, 2 * S - 1)
    for copy in stored:
        copy.wait()
    for copy in pending:
        copy.wait_send()


def on_device(disorder, slice_bounds, start, ritz):
    nc, nx, ny = (lax.axis_size(a) for a in ("cuts", "lx", "ly"))
    count, NV, X, Y, NZ = start.shape
    NR = ritz.shape[1]
    J = X * Y
    S, R, K = count // 2, 2 * Y, ny // 2
    V = pltpu.VMEM
    D = pltpu.SemaphoreType.DMA
    dims = (nc, nx, ny, count, NV, NR, X, Y, NZ)
    hbm = pl.BlockSpec(memory_space=pl.ANY)
    sems = sem_counts(nx, K, S)
    block, corr = pl.pallas_call(
        functools.partial(kernel, dims),
        out_shape=(jax.ShapeDtypeStruct((count, NV * J, NZ), F32),
                   jax.ShapeDtypeStruct((count, 2 * NR, NV), F32)),
        in_specs=[hbm] * 4,
        out_specs=(hbm, hbm),
        scratch_shapes=[
            V((count, NV * J, NZ), F32),
            V((count, 2 * NR, NV), F32),
            pltpu.SMEM((2, count), F32),
            V((J, NZ), jnp.int32),
            V((count, NV * J, NZ), F32),
            V((count, NR * J, NZ), F32),
            D((2 * S + 3,)),
            V((S, X + 2 * H, R + 2 * H, NV, NZ), F32),
            V((S, X, Y, NV, NZ), F32),
            V((X + 2 * H, R + 2 * H, 1, NZ), F32),
            V((S, X + 2 * H, R + 2 * H, NV, NZ), F32),
            V((count, X, Y, NV, NZ), F32),
            V((S, X, Y, NV, NZ), F32),
            V((count + 2, X, Y, NR, NZ), F32),
            V((S + 2, X, Y, NR, NZ), F32),
            V((S, 2 * (NV + 2 * NR), NV + 2 * NR), F32),
            V((S, 2, 8, 128), F32),
            V((nx, S, 2, 8, 128), F32),
            V((S, 2, 8, 128), F32),
            V((K, S, 2, 8, 128), F32),
            V((count, NV, NV + 2 * NR), F32),
            V((S, NV, 128), F32),
            V((S, NV, 128), F32),
            D((sems,)), D((sems,)),
        ],
        compiler_params=pltpu.CompilerParams(collective_id=0, has_side_effects=True, vmem_limit_bytes=48 << 20),
    )(*[pltpu.with_memory_space_constraint(a, pltpu.HBM) for a in (
        disorder.reshape(J, NZ), slice_bounds.T, start.reshape(count, NV * J, NZ), ritz.reshape(count, NR * J, NZ))])
    return (block.reshape(start.shape), corr)


def solution(mesh):
    in_specs = (
        P("lx", "ly", None),
        P("cuts", None),
        P("cuts", None, "lx", "ly", None),
        P("cuts", None, "lx", "ly", None),
    )
    out_specs = (P("cuts", None, "lx", "ly", None), P("cuts", None, None))
    return jax.shard_map(
        on_device, mesh=mesh, in_specs=in_specs, out_specs=out_specs, check_vma=False
    )
```

time: 75.3 us -> 80.2 us (1.065)
  Pallas kernels: 70.7 us -> 77.5 us
  local copies, waits for them, and re-layouts: 3.77 us -> 1.76 us
    pallas_call x1, Pallas kernels: 70.7 us -> 77.5 us  [on_device(): pl.pallas_call(functools.partial(kernel, dims), out_shape=(jax.ShapeDtype...]
    unnamed x4 -> x2, local copies, waits for them, and re-layouts: 3.77 us -> 1.76 us
where the time goes in v2:
time: 80.2 us; the launch traced here: 79.9 us
  Pallas kernels  77.5 us (97%)
  local copies, waits for them, and re-layouts  1.76 us (2%)
    pallas_call x1, Pallas kernels, on_device(): pl.pallas_call(functools.partial(kernel, dims), out_shape=(jax.ShapeDtype...  77.5 us
    unnamed x2, local copies, waits for them, and re-layouts  1.76 us

profile of v2, /device:TPU:0, one launch (start us, length us, event | category | flops | bytes accessed | tf_op | source)
XLA Modules:
  0.0 79.9 jit_solution(17129363343126386536)
XLA Ops:
  0.6 77.5 %shard_map.59 = (f32[6,512,128]{2,1,0:T(8,128)S(1)}, f32[6,16,32]{2,1,0:T(8,128)S(1)}) custom-call(s32[16,128]{1,0:T(8,128)} %bitcast.8, f32[2,6]{1,0:T(2,128)} %bitcast.9, f32[6,512,128]{2,1,0:T(8,128)} %bitcast.6, f32[6,128,128]{2,1,0:T(8,128)} %bitcast.7), custom_call_target="tpu_custom_call" | custom-call | tf_op jit(solution)/shard_map/pallas_call | solution.py:525
  78.2 1.1 %copy.8 = f32[6,32,8,2,128]{4,3,2,1,0:T(2,128)} copy(f32[6,32,8,2,128]{4,3,2,1,0:T(2,128)S(1)} %bitcast.5) | data formatting | bytes 3145728
  79.3 0.6 copy.9

commit v3 on v2

--- a/solution.py
+++ b/solution.py
@@ -65,13 +65,6 @@
         copy.start()
         return copy
 
-    level_load = load(dis_h, dis, 2 * S)
-    bound_load = load(bnd_h, bnd, 2 * S + 2)
-    away, kept = [], []
-    for c in range(S):
-        away.append(load(start_h.at[q * S + c], start.at[c], c))
-        kept.append(load(start_h.at[p * S + c], start.at[S + c], S + c))
-    ritz_load = load(ritz_h, ritz, 2 * S + 1)
     barrier = pltpu.get_barrier_semaphore()
 
     def greet(dev):
@@ -85,15 +78,18 @@
     greet(cup)
     greet(cdown)
 
+    away, kept = [], []
+    for c in range(S):
+        away.append(load(start_h.at[q * S + c], start.at[c], c))
+        kept.append(load(start_h.at[p * S + c], start.at[S + c], S + c))
+        if c == 0:
+            level_load = load(dis_h, dis, 2 * S)
+    bound_load = load(bnd_h, bnd, 2 * S + 2)
+    ritz_load = load(ritz_h, ritz, 2 * S + 1)
+
     lo = H + Y * p
     lq = H + Y * q
     xi = pl.ds(H, X)
-    level_load.wait()
-    for x in range(X):
-        for r in range(Y):
-            row = dis[pl.ds(x * Y + r, 1), :].astype(F32)
-            O[H + x, lo + r] = 16.5 * (row / F32(LEVELS - 1) - 0.5)
-
     def stage_away(c):
         away[c].wait()
         for x in range(X):
@@ -174,11 +170,16 @@
     stage_away(0)
     stage_kept(0)
     pl.semaphore_wait(barrier, nx + K + 1)
-    send(O.at[xi, rows(lo)], O.at[xi, rows(lo)], o_y, o_y, yp)
     send_y(0)
-    send_o(p)
     send_own_z(0)
     send_x(0, xo_at[0], lo)
+    level_load.wait()
+    for x in range(X):
+        for r in range(Y):
+            row = dis[pl.ds(x * Y + r, 1), :].astype(F32)
+            O[H + x, lo + r] = 16.5 * (row / F32(LEVELS - 1) - 0.5)
+    send(O.at[xi, rows(lo)], O.at[xi, rows(lo)], o_y, o_y, yp)
+    send_o(p)
     for c in range(1, S):
         stage_away(c)
         send_y(c)
@@ -195,12 +196,6 @@
     send(RA.at[count], RA.at[0], c_at, c_at, cup)
     send(RA.at[1], RA.at[count + 1], c_at + 1, c_at + 1, cdown)
 
-    own = pl.ds(H, R)
-    arrived(O.at[xi, rows(lq)], o_y)
-    send_o(q)
-    send(O.at[H + X - 1, own], O.at[H - 1, own], o_x, o_x, xup)
-    send(O.at[H, own], O.at[H + X, own], o_x + 1, o_x + 1, xdown)
-
     arrived(RA.at[0], c_at)
     arrived(RA.at[count + 1], c_at + 1)
 
@@ -220,18 +215,16 @@
     for j in order:
         send(RA.at[q * S + j], RQ.at[j], r_at + j, r_at + j, yp)
 
-    for c in range(S):
+    own = pl.ds(H, R)
+
+    def relay_o():
+        arrived(O.at[xi, rows(lq)], o_y)
+        send_o(q)
+        send(O.at[H + X - 1, own], O.at[H - 1, own], o_x, o_x, xup)
+        send(O.at[H, own], O.at[H + X, own], o_x + 1, o_x + 1, xdown)
+
+    def got_y(c):
         arrived(E.at[c, xi, rows(lq)], y_at[c])
-        if c < S - 1:
-            send_rest_z(c)
-        send_x(c, xp_at[c], lq)
-        if c == 0:
-            send_own_z(S - 1)
-
-    arrived(O.at[xi, H - 1], o_z)
-    arrived(O.at[xi, H + R], o_z + 1)
-    arrived(O.at[H - 1, own], o_x)
-    arrived(O.at[H + X, own], o_x + 1)
 
     last = R + 2 * H - 1
     ra = [a + p * (last - 2 * a) for a in range(last + 1)]
@@ -275,10 +268,22 @@
         arrived(E.at[c, xi, rows(jnp.where(p == 1, 0, H + R))], z_at[c])
         corners(c, far, k_at[c])
 
+    def late_corners(c):
+        arrived(E.at[c, xi, ra[near]], z_at[c] + 1)
+        corners(c, near, k_at[c] + 2)
+
+    def got_o():
+        arrived(O.at[xi, H - 1], o_z)
+        arrived(O.at[xi, H + R], o_z + 1)
+        arrived(O.at[H - 1, own], o_x)
+        arrived(O.at[H + X, own], o_x + 1)
+
     def early(c):
         one, two = refs(c)
         got_x(c, xo_at[c], lo)
         got_x(c, xp_at[c], lq)
+        if c == 0:
+            got_o()
 
         def inner(i):
             for a in range(H + 1, far + 1):
@@ -306,8 +311,6 @@
 
     def late(c):
         one, two = refs(c)
-        arrived(E.at[c, xi, ra[near]], z_at[c] + 1)
-        corners(c, near, k_at[c] + 2)
         arrived(E.at[c, xi, ra[near - 1]], z_at[c] + 2)
 
         def inner(i):
@@ -354,10 +357,16 @@
         g = g[:NB] + (cross + cross.T)[:NB]
         lane = lax.broadcasted_iota(jnp.int32, (8, 128), 1)
         t0 = jnp.zeros((8, 128), F32)
+        t1 = jnp.zeros((8, 128), F32)
         for b_ in range(NV // 8):
-            piece = jnp.where(lane < NV, g[b_ * 8:b_ * 8 + 8], 0.0)
-            t0 = t0 + (pltpu.roll(piece, b_ * NV, 1) if b_ else piece)
-        t1 = g[NV:NV + 8] + pltpu.roll(g[NV + 8:NV + 16], 64, 1)
+            block = g[b_ * 8:b_ * 8 + 8]
+            ff = jnp.where(lane < NV, block, 0.0)
+            fw = jnp.where(lane >= NV, block, 0.0)
+            t0 = t0 + (pltpu.roll(ff, b_ * NV, 1) if b_ else ff)
+            t1 = t1 + pltpu.roll(fw, (128 - NV + b_ * NW) % 128, 1)
+        for b_ in range(NW // 8):
+            ww = jnp.where(lane >= NV, g[NV + b_ * 8:NV + b_ * 8 + 8], 0.0)
+            t1 = t1 + pltpu.roll(ww, (128 - NV + (NV // 8 + b_) * NW) % 128, 1)
         PK[c, 0] = t0
         PK[c, 1] = t1
 
@@ -386,7 +395,6 @@
     l32 = lax.broadcasted_iota(jnp.int32, (NV, 128), 1)
     r32 = lax.broadcasted_iota(jnp.int32, (NV, 128), 0)
     eye = jnp.where(l32 == r32 + NV, 1.0, 0.0)
-    ident = jnp.where(l32 == r32, 1.0, 0.0)[:, :NV]
 
     def factor(c):
         for o in range(1, K):
@@ -397,24 +405,31 @@
             acc = acc + RZ[t, c]
         acc = acc * (1.0 / total)
         t0, t1 = acc[0], acc[1]
-        ff = jnp.concatenate([pltpu.roll(t0, 128 - b * NV, 1) if b else t0 for b in range(NV // 8)], 0)
-        w = jnp.concatenate([t1, pltpu.roll(t1, 64, 1)], 0)
-        corr = w[:, :NV]
-        b = jnp.where(e16r == e16l, 2.0, 0.0) - pltpu.roll(w, 128 - NV, 1)[:, :NW]
-        bc = lax.dot_general(b, corr, NN, precision=HP, preferred_element_type=F32)
-        sub = lax.dot_general(corr, bc, TN, precision=HP, preferred_element_type=F32)
+
+        def strip(t, at):
+            return pltpu.roll(t, 128 - at, 1) if at else t
+
+        ff = jnp.concatenate([strip(t0, b * NV) for b in range(NV // 8)], 0)
+        fw = jnp.concatenate([strip(t1, b * NW) for b in range(NV // 8)], 0)
+        ww = jnp.concatenate([strip(t1, NV // 8 * NW + b * NW) for b in range(NW // 8)], 0)
+        b = jnp.where(e16r == e16l, 2.0, 0.0) - ww[:, :NW]
+        fn = fw[:, :NW]
+        fb = lax.dot_general(fn, b, NN, precision=HP, preferred_element_type=F32)
+        sub = lax.dot_general(fb, fn, NT, precision=HP, preferred_element_type=F32)
         sub = jnp.concatenate([sub, jnp.zeros((NV, 128 - NV), F32)], 1)
         M = jnp.where(l32 < NV, ff - sub, eye)
+        wide = jnp.where(l32 < NW, fw, 0.0)
+        M = M - pltpu.roll(wide, 2 * NV, 1)
         line = lax.broadcasted_iota(jnp.int32, (NV, 1), 0)
         for j in range(0, NV, 2):
             r0, r1 = M[j:j + 1], M[j + 1:j + 2]
-            c0, c1 = M[:, j:j + 1], M[:, j + 1:j + 2]
+            c0 = jnp.broadcast_to(M[:, j:j + 1], (NV, 128))
+            c1 = jnp.broadcast_to(M[:, j + 1:j + 2], (NV, 128))
             p00, p01, p11 = c0[j:j + 1], c1[j:j + 1], c1[j + 1:j + 2]
             inv = 1.0 / (p00 * p11 - p01 * p01)
-            keep = jnp.where(line > j + 1, inv, 0.0)
-            f0 = (c0 * p11 - c1 * p01) * keep
-            f1 = (c1 * p00 - c0 * p01) * keep
-            M = M - f0 * r0 - f1 * r1
+            g0 = (p11 * r0 - p01 * r1) * inv
+            g1 = (p00 * r1 - p01 * r0) * inv
+            M = jnp.where(line > j + 1, M - c0 * g0 - c1 * g1, M)
         odd = r32 % 2
         diag = jnp.sum(jnp.where(l32 == r32, M, 0.0), axis=1, keepdims=True)
         side = jnp.sum(jnp.where(l32 == r32 - odd, M, 0.0), axis=1, keepdims=True)
@@ -424,22 +439,21 @@
         diag = jnp.sum(jnp.where(l32 == r32, M, 0.0), axis=1, keepdims=True)
         M = M * (1.0 / jnp.sqrt(diag))
         s = p * S + c
-        linv = pltpu.roll(M, 128 - NV, 1)[:, :NV]
-        full = jnp.concatenate([ident, -corr], 0)
-        lm = lax.dot_general(linv, full, NT, precision=HP, preferred_element_type=F32)
-        wide = jnp.concatenate([corr, jnp.zeros((NV - NW, NV), F32)], 0)
-        wide = jnp.concatenate([lm, jnp.zeros((NV, 64 - NB), F32), wide, jnp.zeros((NV, 64 - NV), F32)], 1)
-        LP[c] = wide
+        M = pltpu.roll(M, 128 - NV, 1)
+        LP[c] = jnp.where(l32 < NB, M, pltpu.roll(wide, 2 * NV, 1))
         send(LP.at[c], LR.at[c], l_at[c], l_at[c], yp)
-        LM[s] = lm
-        cor[s] = corr
+        LM[s] = M[:, :NB]
+        keep_corr(s, wide)
+
+    def keep_corr(s, wide):
+        cor[s] = jnp.concatenate([wide, jnp.zeros((128 - NV, 128), F32)], 0).T[:NW, :NV]
 
     def take(c):
         s = q * S + c
         arrived(LR.at[c], l_at[c])
         wide = LR[c]
         LM[s] = wide[:, :NB]
-        cor[s] = pltpu.roll(wide, 64, 1)[:NW, :NV]
+        keep_corr(s, pltpu.roll(wide, 128 - 2 * NV, 1))
         arrived(FA.at[s], f_at[c])
 
     stored = []
@@ -470,38 +484,53 @@
         take(c)
         finish(q * S + c, S + c)
 
-    early_corners(0)
-    early(0)
+    end = S - 1
+    for c in range(S):
+        got_y(c)
+        if c < end:
+            send_rest_z(c)
+        send_x(c, xp_at[c], lq)
+        if c == 0:
+            send_own_z(end)
+            relay_o()
+            early_corners(0)
+        if c == 1:
+            early(0)
+            early_corners(1) if c < end else None
+    for c in range(1, end):
+        early(c)
+    late_corners(0)
+    gram_rest(0)
     late(0)
-    gram_rest(0)
     gram_own(0)
     sum_x_start(0)
-    for c in range(1, S):
-        early_corners(c) if c < S - 1 else None
-    for c in range(1, S):
-        if c == S - 1:
-            sum_x_end(0)
-            send_rest_z(c)
-            early_corners(c)
-        early(c)
+    for c in range(1, end):
         gram_rest(c)
-    for c in range(1, S - 1):
+    early_corners(end)
+    sum_x_end(0)
+    send_rest_z(end)
+    early(end)
+    gram_rest(end)
+    for c in range(1, end):
+        late_corners(c)
         late(c)
         gram_own(c)
         sum_x_start(c)
         factor(c - 1)
         finish_own(c - 1)
         sum_x_end(c)
-        finish_rest(c - 1)
-    late(S - 1)
-    gram_own(S - 1)
-    sum_x_start(S - 1)
-    sum_x_end(S - 1)
-    factor(S - 2)
-    finish_own(S - 2)
-    factor(S - 1)
-    finish_rest(S - 2)
-    finish_own(S - 1)
+    late_corners(end)
+    late(end)
+    gram_own(end)
+    sum_x_start(end)
+    sum_x_end(end)
+    factor(end - 1)
+    finish_own(end - 1)
+    factor(end)
+    for c in range(end - 1):
+        finish_rest(c)
+    finish_own(end)
+    finish_rest(end - 1)
     take(S - 1)
     store(cor, cor_h, 2 * S)
     finish(q * S + S - 1, 2 * S - 1)

time: 80.2 us -> 72.9 us (0.909)
  Pallas kernels: 77.5 us -> 70.3 us
    pallas_call x1, Pallas kernels: 77.5 us -> 70.3 us  [on_device(): pl.pallas_call(functools.partial(kernel, dims), out_shape=(jax.ShapeDtype...]
where the time goes in v3:
time: 72.9 us; the launch traced here: 72.7 us
  Pallas kernels  70.3 us (96%)
  local copies, waits for them, and re-layouts  1.76 us (2%)
    pallas_call x1, Pallas kernels, on_device(): pl.pallas_call(functools.partial(kernel, dims), out_shape=(jax.ShapeDtype...  70.3 us
    unnamed x2, local copies, waits for them, and re-layouts  1.76 us

profile of v3, /device:TPU:0, one launch (start us, length us, event | category | flops | bytes accessed | tf_op | source)
XLA Modules:
  0.0 72.7 jit_solution(17825114977004915217)
XLA Ops:
  0.6 70.3 %shard_map.59 = (f32[6,512,128]{2,1,0:T(8,128)S(1)}, f32[6,16,32]{2,1,0:T(8,128)S(1)}) custom-call(s32[16,128]{1,0:T(8,128)} %bitcast.8, f32[2,6]{1,0:T(2,128)} %bitcast.9, f32[6,512,128]{2,1,0:T(8,128)} %bitcast.6, f32[6,128,128]{2,1,0:T(8,128)} %bitcast.7), custom_call_target="tpu_custom_call" | custom-call | tf_op jit(solution)/shard_map/pallas_call | solution.py:554
  71.0 1.1 %copy.8 = f32[6,32,8,2,128]{4,3,2,1,0:T(2,128)} copy(f32[6,32,8,2,128]{4,3,2,1,0:T(2,128)S(1)} %bitcast.5) | data formatting | bytes 3145728
  72.1 0.6 copy.9

commit v4 on v3

--- a/solution.py
+++ b/solution.py
@@ -78,12 +78,11 @@
     greet(cup)
     greet(cdown)
 
+    level_load = load(dis_h, dis, 2 * S)
     away, kept = [], []
     for c in range(S):
         away.append(load(start_h.at[q * S + c], start.at[c], c))
         kept.append(load(start_h.at[p * S + c], start.at[S + c], S + c))
-        if c == 0:
-            level_load = load(dis_h, dis, 2 * S)
     bound_load = load(bnd_h, bnd, 2 * S + 2)
     ritz_load = load(ritz_h, ritz, 2 * S + 1)
 
@@ -167,23 +166,33 @@
         dst = jnp.where(half == 1, 1, H + R)
         send(O.at[xi, src], O.at[xi, dst], o_z + side, o_z + side, dev)
 
-    stage_away(0)
-    stage_kept(0)
-    pl.semaphore_wait(barrier, nx + K + 1)
-    send_y(0)
-    send_own_z(0)
-    send_x(0, xo_at[0], lo)
+    own = pl.ds(H, R)
+
+    def relay_o():
+        arrived(O.at[xi, rows(lq)], o_y)
+        send_o(q)
+        send(O.at[H + X - 1, own], O.at[H - 1, own], o_x, o_x, xup)
+        send(O.at[H, own], O.at[H + X, own], o_x + 1, o_x + 1, xdown)
+
     level_load.wait()
     for x in range(X):
         for r in range(Y):
             row = dis[pl.ds(x * Y + r, 1), :].astype(F32)
             O[H + x, lo + r] = 16.5 * (row / F32(LEVELS - 1) - 0.5)
+    stage_away(0)
+    stage_kept(0)
+    pl.semaphore_wait(barrier, nx + K + 1)
     send(O.at[xi, rows(lo)], O.at[xi, rows(lo)], o_y, o_y, yp)
+    send_y(0)
     send_o(p)
+    send_own_z(0)
+    send_x(0, xo_at[0], lo)
     for c in range(1, S):
         stage_away(c)
         send_y(c)
         stage_kept(c)
+        if c == 1:
+            relay_o()
         if c < S - 1:
             send_own_z(c)
         send_x(c, xo_at[c], lo)
@@ -214,14 +223,6 @@
                 order.append(j)
     for j in order:
         send(RA.at[q * S + j], RQ.at[j], r_at + j, r_at + j, yp)
-
-    own = pl.ds(H, R)
-
-    def relay_o():
-        arrived(O.at[xi, rows(lq)], o_y)
-        send_o(q)
-        send(O.at[H + X - 1, own], O.at[H - 1, own], o_x, o_x, xup)
-        send(O.at[H, own], O.at[H + X, own], o_x + 1, o_x + 1, xdown)
 
     def got_y(c):
         arrived(E.at[c, xi, rows(lq)], y_at[c])
@@ -492,14 +493,15 @@
         send_x(c, xp_at[c], lq)
         if c == 0:
             send_own_z(end)
-            relay_o()
             early_corners(0)
         if c == 1:
+            early_corners(1) if c < end else None
             early(0)
-            early_corners(1) if c < end else None
+    for c in range(2, end):
+        early_corners(c)
+    late_corners(0)
     for c in range(1, end):
         early(c)
-    late_corners(0)
     gram_rest(0)
     late(0)
     gram_own(0)
@@ -510,16 +512,18 @@
     sum_x_end(0)
     send_rest_z(end)
     early(end)
+    for c in range(1, end):
+        late_corners(c)
     gram_rest(end)
     for c in range(1, end):
-        late_corners(c)
         late(c)
         gram_own(c)
         sum_x_start(c)
         factor(c - 1)
+        if c == end - 1:
+            late_corners(end)
         finish_own(c - 1)
         sum_x_end(c)
-    late_corners(end)
     late(end)
     gram_own(end)
     sum_x_start(end)

time: 72.9 us -> 64.8 us (0.89)
  Pallas kernels: 70.3 us -> 62.2 us
    pallas_call x1, Pallas kernels: 70.3 us -> 62.2 us  [on_device(): pl.pallas_call(functools.partial(kernel, dims), out_shape=(jax.ShapeDtype...]
where the time goes in v4:
time: 64.8 us; the launch traced here: 64.6 us
  Pallas kernels  62.2 us (96%)
  local copies, waits for them, and re-layouts  1.76 us (3%)
    pallas_call x1, Pallas kernels, on_device(): pl.pallas_call(functools.partial(kernel, dims), out_shape=(jax.ShapeDtype...  62.2 us
    unnamed x2, local copies, waits for them, and re-layouts  1.76 us

profile of v4, /device:TPU:0, one launch (start us, length us, event | category | flops | bytes accessed | tf_op | source)
XLA Modules:
  0.0 64.6 jit_solution(14721404259912368736)
XLA Ops:
  0.6 62.2 %shard_map.59 = (f32[6,512,128]{2,1,0:T(8,128)S(1)}, f32[6,16,32]{2,1,0:T(8,128)S(1)}) custom-call(s32[16,128]{1,0:T(8,128)} %bitcast.8, f32[2,6]{1,0:T(2,128)} %bitcast.9, f32[6,512,128]{2,1,0:T(8,128)} %bitcast.6, f32[6,128,128]{2,1,0:T(8,128)} %bitcast.7), custom_call_target="tpu_custom_call" | custom-call | tf_op jit(solution)/shard_map/pallas_call | solution.py:558
  62.9 1.1 %copy.8 = f32[6,32,8,2,128]{4,3,2,1,0:T(2,128)} copy(f32[6,32,8,2,128]{4,3,2,1,0:T(2,128)S(1)} %bitcast.5) | data formatting | bytes 3145728
  64.0 0.6 copy.9

commit v5 on v4

--- a/solution.py
+++ b/solution.py
@@ -18,8 +18,12 @@
 TN = (((0,), (0,)), ((), ()))
 
 
+def direct_sum(nx, K):
+    return nx * K <= 16
+
+
 def sem_counts(nx, K, S):
-    return 5 + S * (14 + nx + K) + 2 + (S + 2)
+    return 5 + S * 14 + 2 + (S + 2) + 2 * (nx * K if direct_sum(nx, K) else nx + K)
 
 
 def split(z):
@@ -71,10 +75,17 @@
         pl.semaphore_signal(barrier, inc=1, device_id=dev, device_id_type=MESH)
 
     greet(yp)
-    for o in range(1, nx):
-        greet((cut, lax.rem(mx + o, nx), my))
-    for o in range(1, K):
-        greet((cut, mx, lax.rem(kz + o, K) * 2 + p))
+    if direct_sum(nx, K):
+        for o in range(1, nx * K):
+            t = lax.rem(mx * K + kz + o, nx * K)
+            greet((cut, t // K, lax.rem(t, K) * 2 + p))
+        greeted = nx * K + 2
+    else:
+        for o in range(1, nx):
+            greet((cut, lax.rem(mx + o, nx), my))
+        for o in range(1, K):
+            greet((cut, mx, lax.rem(kz + o, K) * 2 + p))
+        greeted = nx + K + 1
     greet(cup)
     greet(cdown)
 
@@ -114,6 +125,11 @@
             src_ref=src, dst_ref=dst, send_sem=ss.at[i], recv_sem=rs.at[j], device_id=dev, device_id_type=MESH)
         copy.start()
         pending.append(copy)
+
+    def flush(n):
+        for copy in pending[:n]:
+            copy.wait_send()
+        del pending[:n]
 
     def arrived(dst, j):
         pltpu.make_async_remote_copy(
@@ -133,8 +149,12 @@
     l_at = [slots() for _ in range(S)]
     c_at = slots(2)
     r_at = slots(S + 2)
-    ax_at = [slots(nx) for _ in range(S)]
-    az_at = [slots(K) for _ in range(S)]
+    groups = [list(range(S - 1)), [S - 1]]
+    direct = direct_sum(nx, K)
+    span = nx * K if direct else K
+    me = mx * K + kz if direct else kz
+    ax_at = [0 if direct else slots(nx) for _ in groups]
+    az_at = [slots(span) for _ in groups]
 
     def send_y(c):
         send(T.at[c], E.at[c, xi, rows(lo)], y_at[c], y_at[c], yp)
@@ -181,7 +201,7 @@
             O[H + x, lo + r] = 16.5 * (row / F32(LEVELS - 1) - 0.5)
     stage_away(0)
     stage_kept(0)
-    pl.semaphore_wait(barrier, nx + K + 1)
+    pl.semaphore_wait(barrier, greeted)
     send(O.at[xi, rows(lo)], O.at[xi, rows(lo)], o_y, o_y, yp)
     send_y(0)
     send_o(p)
@@ -327,18 +347,28 @@
         for x in (H - 1, H + X):
             one(x, H)
 
-        def outer(i):
-            for a in range(H, H + Y):
-                FA[p * S + c, i, ra[a] - lo] = two(H + i, a)
-
-        loop(X, 2, outer)
+        s = p * S + c
+
+        def outer(i, acc):
+            for k in range(2):
+                x = 2 * i + k
+                for a in range(H, H + Y):
+                    FA[s, x, ra[a] - lo] = two(H + x, a)
+                z = [jnp.concatenate([FA[s, x, r], RA[s, x, r], RA[s + 2, x, r]], 0) for r in range(Y)]
+                acc = acc + square(z)
+            return acc
+
+        gram_pack(c, lax.fori_loop(0, X // 2, outer, GS[c]))
+
+    def square(z):
+        hi, lw = split(jnp.concatenate(z, 1))
+        return lax.dot_general(jnp.concatenate([hi, lw], 0), hi, NT, preferred_element_type=F32)
 
     def product(f, w0, w1):
         def body(i, acc):
             for k in range(2):
                 z = [jnp.concatenate([f(2 * i + k, r), w0(2 * i + k, r), w1(2 * i + k, r)], 0) for r in range(Y)]
-                hi, lw = split(jnp.concatenate(z, 1))
-                acc = acc + lax.dot_general(jnp.concatenate([hi, lw], 0), hi, NT, preferred_element_type=F32)
+                acc = acc + square(z)
             return acc
 
         return lax.fori_loop(0, X // 2, body, jnp.zeros((2 * NB, NB), F32))
@@ -350,9 +380,7 @@
                 seen.add(j)
         GS[c] = product(lambda x, r: FT[c, x, r], lambda x, r: RQ[c, x, r], lambda x, r: RQ[c + 2, x, r])
 
-    def gram_own(c):
-        s = p * S + c
-        g = GS[c] + product(lambda x, r: FA[s, x, r], lambda x, r: RA[s, x, r], lambda x, r: RA[s + 2, x, r])
+    def gram_pack(c, g):
         g = jnp.concatenate([g, jnp.zeros((2 * NB, 128 - NB), F32)], 1)
         cross = jnp.concatenate([g[NB:], jnp.zeros((128 - NB, 128), F32)], 0)
         g = g[:NB] + (cross + cross.T)[:NB]
@@ -373,23 +401,43 @@
 
     seen = set()
 
-    def sum_x_start(c):
-        RX[mx, c] = PK[c]
+    def spread(k, src):
+        cs = groups[k]
+        part = pl.ds(cs[0], len(cs))
+        for o in range(1, span):
+            t = lax.rem(me + o, span)
+            x, z = (t // K, lax.rem(t, K)) if direct else (mx, t)
+            send(src.at[part], RZ.at[me, part], az_at[k] + o, az_at[k] + me, (cut, x, z * 2 + p))
+
+    def sum_start(k):
+        cs = groups[k]
+        part = pl.ds(cs[0], len(cs))
+        for c in cs:
+            if direct:
+                RZ[me, c] = PK[c]
+            else:
+                RX[mx, c] = PK[c]
+        if direct:
+            spread(k, PK)
+            return
         for o in range(1, nx):
-            send(PK.at[c], RX.at[mx, c], ax_at[c] + o, ax_at[c] + mx, (cut, lax.rem(mx + o, nx), my))
-
-    def sum_x_end(c):
+            send(PK.at[part], RX.at[mx, part], ax_at[k] + o, ax_at[k] + mx, (cut, lax.rem(mx + o, nx), my))
+
+    def sum_more(k):
+        if direct:
+            return
+        cs = groups[k]
+        part = pl.ds(cs[0], len(cs))
         for o in range(1, nx):
             t = lax.rem(mx + o, nx)
-            arrived(RX.at[t, c], ax_at[c] + t)
-        acc = RX[0, c]
-        for t in range(1, nx):
-            acc = acc + RX[t, c]
-        SM[c] = acc
-        RZ[kz, c] = acc
-        for o in range(1, K):
-            t = lax.rem(kz + o, K)
-            send(SM.at[c], RZ.at[kz, c], az_at[c] + o, az_at[c] + kz, (cut, mx, t * 2 + p))
+            arrived(RX.at[t, part], ax_at[k] + t)
+        for c in cs:
+            acc = RX[0, c]
+            for t in range(1, nx):
+                acc = acc + RX[t, c]
+            SM[c] = acc
+            RZ[kz, c] = acc
+        spread(k, SM)
 
     e16r = lax.broadcasted_iota(jnp.int32, (NW, NW), 0)
     e16l = lax.broadcasted_iota(jnp.int32, (NW, NW), 1)
@@ -397,19 +445,18 @@
     r32 = lax.broadcasted_iota(jnp.int32, (NV, 128), 0)
     eye = jnp.where(l32 == r32 + NV, 1.0, 0.0)
 
-    def factor(c):
-        for o in range(1, K):
-            t = lax.rem(kz + o, K)
-            arrived(RZ.at[t, c], az_at[c] + t)
+    line = lax.broadcasted_iota(jnp.int32, (NV, 1), 0)
+    odd = r32 % 2
+
+    def strip(t, at):
+        return pltpu.roll(t, 128 - at, 1) if at else t
+
+    def cleaned(c):
         acc = RZ[0, c]
-        for t in range(1, K):
+        for t in range(1, span):
             acc = acc + RZ[t, c]
         acc = acc * (1.0 / total)
         t0, t1 = acc[0], acc[1]
-
-        def strip(t, at):
-            return pltpu.roll(t, 128 - at, 1) if at else t
-
         ff = jnp.concatenate([strip(t0, b * NV) for b in range(NV // 8)], 0)
         fw = jnp.concatenate([strip(t1, b * NW) for b in range(NV // 8)], 0)
         ww = jnp.concatenate([strip(t1, NV // 8 * NW + b * NW) for b in range(NW // 8)], 0)
@@ -418,33 +465,44 @@
         fb = lax.dot_general(fn, b, NN, precision=HP, preferred_element_type=F32)
         sub = lax.dot_general(fb, fn, NT, precision=HP, preferred_element_type=F32)
         sub = jnp.concatenate([sub, jnp.zeros((NV, 128 - NV), F32)], 1)
-        M = jnp.where(l32 < NV, ff - sub, eye)
         wide = jnp.where(l32 < NW, fw, 0.0)
-        M = M - pltpu.roll(wide, 2 * NV, 1)
-        line = lax.broadcasted_iota(jnp.int32, (NV, 1), 0)
-        for j in range(0, NV, 2):
-            r0, r1 = M[j:j + 1], M[j + 1:j + 2]
-            c0 = jnp.broadcast_to(M[:, j:j + 1], (NV, 128))
-            c1 = jnp.broadcast_to(M[:, j + 1:j + 2], (NV, 128))
-            p00, p01, p11 = c0[j:j + 1], c1[j:j + 1], c1[j + 1:j + 2]
-            inv = 1.0 / (p00 * p11 - p01 * p01)
-            g0 = (p11 * r0 - p01 * r1) * inv
-            g1 = (p00 * r1 - p01 * r0) * inv
-            M = jnp.where(line > j + 1, M - c0 * g0 - c1 * g1, M)
-        odd = r32 % 2
+        return jnp.where(l32 < NV, ff - sub, eye) - pltpu.roll(wide, 2 * NV, 1), wide
+
+    def eliminate(M, j):
+        r0, r1 = M[j:j + 1], M[j + 1:j + 2]
+        c0 = jnp.broadcast_to(M[:, j:j + 1], (NV, 128))
+        c1 = jnp.broadcast_to(M[:, j + 1:j + 2], (NV, 128))
+        p00, p01, p11 = c0[j:j + 1], c1[j:j + 1], c1[j + 1:j + 2]
+        inv = 1.0 / (p00 * p11 - p01 * p01)
+        g0 = (p11 * r0 - p01 * r1) * inv
+        g1 = (p00 * r1 - p01 * r0) * inv
+        return jnp.where(line > j + 1, M - c0 * g0 - c1 * g1, M)
+
+    def scaled(M):
         diag = jnp.sum(jnp.where(l32 == r32, M, 0.0), axis=1, keepdims=True)
         side = jnp.sum(jnp.where(l32 == r32 - odd, M, 0.0), axis=1, keepdims=True)
-        above = pltpu.roll(M, 1, 0)
         ratio = side / pltpu.roll(jnp.broadcast_to(diag, (NV, 128)), 1, 0)
-        M = jnp.where(odd == 1, M - ratio * above, M)
+        M = jnp.where(odd == 1, M - ratio * pltpu.roll(M, 1, 0), M)
         diag = jnp.sum(jnp.where(l32 == r32, M, 0.0), axis=1, keepdims=True)
-        M = M * (1.0 / jnp.sqrt(diag))
-        s = p * S + c
-        M = pltpu.roll(M, 128 - NV, 1)
-        LP[c] = jnp.where(l32 < NB, M, pltpu.roll(wide, 2 * NV, 1))
-        send(LP.at[c], LR.at[c], l_at[c], l_at[c], yp)
-        LM[s] = M[:, :NB]
-        keep_corr(s, wide)
+        return pltpu.roll(M * (1.0 / jnp.sqrt(diag)), 128 - NV, 1)
+
+    def factor(k):
+        cs = groups[k]
+        part = pl.ds(cs[0], len(cs))
+        for o in range(1, span):
+            t = lax.rem(me + o, span)
+            arrived(RZ.at[t, part], az_at[k] + t)
+        both = [cleaned(c) for c in cs]
+        mats = [m for m, _ in both]
+        for j in range(0, NV, 2):
+            mats = [eliminate(m, j) for m in mats]
+        mats = [scaled(m) for m in mats]
+        for i, c in enumerate(cs):
+            LP[c] = jnp.where(l32 < NB, mats[i], pltpu.roll(both[i][1], 2 * NV, 1))
+            send(LP.at[c], LR.at[c], l_at[c], l_at[c], yp)
+        for i, c in enumerate(cs):
+            LM[p * S + c] = mats[i][:, :NB]
+            keep_corr(p * S + c, both[i][1])
 
     def keep_corr(s, wide):
         cor[s] = jnp.concatenate([wide, jnp.zeros((128 - NV, 128), F32)], 0).T[:NW, :NV]
@@ -488,8 +546,7 @@
     end = S - 1
     for c in range(S):
         got_y(c)
-        if c < end:
-            send_rest_z(c)
+        send_rest_z(c)
         send_x(c, xp_at[c], lq)
         if c == 0:
             send_own_z(end)
@@ -497,6 +554,7 @@
         if c == 1:
             early_corners(1) if c < end else None
             early(0)
+            mark = len(pending)
     for c in range(2, end):
         early_corners(c)
     late_corners(0)
@@ -504,44 +562,37 @@
         early(c)
     gram_rest(0)
     late(0)
-    gram_own(0)
-    sum_x_start(0)
+    early_corners(end)
+    flush(mark // 2)
     for c in range(1, end):
         gram_rest(c)
-    early_corners(end)
-    sum_x_end(0)
-    send_rest_z(end)
     early(end)
     for c in range(1, end):
         late_corners(c)
     gram_rest(end)
     for c in range(1, end):
         late(c)
-        gram_own(c)
-        sum_x_start(c)
-        factor(c - 1)
-        if c == end - 1:
-            late_corners(end)
-        finish_own(c - 1)
-        sum_x_end(c)
+    sum_start(0)
+    flush(mark - mark // 2)
+    late_corners(end)
+    sum_more(0)
     late(end)
-    gram_own(end)
-    sum_x_start(end)
-    sum_x_end(end)
-    factor(end - 1)
-    finish_own(end - 1)
-    factor(end)
-    for c in range(end - 1):
+    sum_start(1)
+    sum_more(1)
+    factor(0)
+    for c in range(end):
+        finish_own(c)
+    factor(1)
+    for c in range(end):
         finish_rest(c)
     finish_own(end)
-    finish_rest(end - 1)
+    flush(len(pending) - 1)
     take(S - 1)
     store(cor, cor_h, 2 * S)
     finish(q * S + S - 1, 2 * S - 1)
     for copy in stored:
         copy.wait()
-    for copy in pending:
-        copy.wait_send()
+    flush(len(pending))
 
 
 def on_device(disorder, slice_bounds, start, ritz):
@@ -581,7 +632,7 @@
             V((S, 2, 8, 128), F32),
             V((nx, S, 2, 8, 128), F32),
             V((S, 2, 8, 128), F32),
-            V((K, S, 2, 8, 128), F32),
+            V((nx * K if direct_sum(nx, K) else K, S, 2, 8, 128), F32),
             V((count, NV, NV + 2 * NR), F32),
             V((S, NV, 128), F32),
             V((S, NV, 128), F32),

time: 64.8 us -> 59.3 us (0.915)
  Pallas kernels: 62.2 us -> 56.6 us
    pallas_call x1, Pallas kernels: 62.2 us -> 56.6 us  [on_device(): pl.pallas_call(functools.partial(kernel, dims), out_shape=(jax.ShapeDtype...]
where the time goes in v5:
time: 59.3 us; the launch traced here: 59 us
  Pallas kernels  56.6 us (95%)
  local copies, waits for them, and re-layouts  1.76 us (3%)
  between operations  0.64 us (1%)
    pallas_call x1, Pallas kernels, on_device(): pl.pallas_call(functools.partial(kernel, dims), out_shape=(jax.ShapeDtype...  56.6 us
    unnamed x2, local copies, waits for them, and re-layouts  1.76 us

profile of v5, /device:TPU:0, one launch (start us, length us, event | category | flops | bytes accessed | tf_op | source)
XLA Modules:
  0.0 59.0 jit_solution(4178595412200792476)
XLA Ops:
  0.6 56.6 %shard_map.59 = (f32[6,512,128]{2,1,0:T(8,128)S(1)}, f32[6,16,32]{2,1,0:T(8,128)S(1)}) custom-call(s32[16,128]{1,0:T(8,128)} %bitcast.8, f32[2,6]{1,0:T(2,128)} %bitcast.9, f32[6,512,128]{2,1,0:T(8,128)} %bitcast.6, f32[6,128,128]{2,1,0:T(8,128)} %bitcast.7), custom_call_target="tpu_custom_call" | custom-call | tf_op jit(solution)/shard_map/pallas_call | solution.py:609
  57.3 1.1 %copy.8 = f32[6,32,8,2,128]{4,3,2,1,0:T(2,128)} copy(f32[6,32,8,2,128]{4,3,2,1,0:T(2,128)S(1)} %bitcast.5) | data formatting | bytes 3145728
  58.4 0.6 %copy.9 = f32[6,16,32]{2,1,0:T(8,128)} copy(f32[6,16,32]{2,1,0:T(8,128)S(1)} %get-tuple-element.9) | data formatting | bytes 24576

commit v6 on v5

--- a/solution.py
+++ b/solution.py
@@ -23,7 +23,8 @@
 
 
 def sem_counts(nx, K, S):
-    return 5 + S * 14 + 2 + (S + 2) + 2 * (nx * K if direct_sum(nx, K) else nx + K)
+    more = 0 if direct_sum(nx, K) else 2
+    return 12 + 3 * S + more, 9 + 11 * S + more
 
 
 def split(z):
@@ -100,6 +101,7 @@
     lo = H + Y * p
     lq = H + Y * q
     xi = pl.ds(H, X)
+    mid = pl.ds(H + 1, X - 2)
     def stage_away(c):
         away[c].wait()
         for x in range(X):
@@ -112,24 +114,21 @@
             for r in range(Y):
                 E[c, H + x, lo + r] = start[S + c, pl.ds(x * Y + r, NV, stride=J), :]
 
-    pending = []
-    used = [0]
-
-    def slots(n=1):
-        i = used[0]
-        used[0] += n
+    used = [0, 0]
+
+    def take_slots(kind, n=1):
+        i = used[kind]
+        used[kind] += n
         return i
 
     def send(src, dst, i, j, dev):
-        copy = pltpu.make_async_remote_copy(
-            src_ref=src, dst_ref=dst, send_sem=ss.at[i], recv_sem=rs.at[j], device_id=dev, device_id_type=MESH)
-        copy.start()
-        pending.append(copy)
-
-    def flush(n):
-        for copy in pending[:n]:
-            copy.wait_send()
-        del pending[:n]
+        pltpu.make_async_remote_copy(
+            src_ref=src, dst_ref=dst, send_sem=ss.at[i], recv_sem=rs.at[j], device_id=dev, device_id_type=MESH).start()
+
+    def left(src, i):
+        pltpu.make_async_remote_copy(
+            src_ref=src, dst_ref=src, send_sem=ss.at[i], recv_sem=ss.at[i],
+            device_id=yp, device_id_type=MESH).wait_send()
 
     def arrived(dst, j):
         pltpu.make_async_remote_copy(
@@ -139,60 +138,54 @@
     def rows(at):
         return pl.ds(at, Y)
 
-    o_y, o_z, o_x = slots(), slots(2), slots(2)
-    y_at = [slots() for _ in range(S)]
-    z_at = [slots(3) for _ in range(S)]
-    xo_at = [slots(2) for _ in range(S)]
-    xp_at = [slots(2) for _ in range(S)]
-    k_at = [slots(4) for _ in range(S)]
-    f_at = [slots() for _ in range(S)]
-    l_at = [slots() for _ in range(S)]
-    c_at = slots(2)
-    r_at = slots(S + 2)
+    so, sy, sf, sl, sr, sc = (take_slots(0, n) for n in (5, 1, 1, 1, 1, 1))
+    sz, sx, sk, sa = (take_slots(0, n) for n in (S, S, S, 2))
+    ro, ry, rf, rl, rx, rc, rr, ra_ = (take_slots(1, n) for n in (5, S, S, S, S, 2, S, 2))
+    rz, rk = take_slots(1, 4 * S), take_slots(1, 2 * S)
     groups = [list(range(S - 1)), [S - 1]]
     direct = direct_sum(nx, K)
     span = nx * K if direct else K
     me = mx * K + kz if direct else kz
-    ax_at = [0 if direct else slots(nx) for _ in groups]
-    az_at = [slots(span) for _ in groups]
+    sb, rb = (0, 0) if direct else (take_slots(0, 2), take_slots(1, 2))
 
     def send_y(c):
-        send(T.at[c], E.at[c, xi, rows(lo)], y_at[c], y_at[c], yp)
+        send(T.at[c], E.at[c, xi, rows(lo)], sy, ry + c, yp)
+
+    def z_dev(half):
+        return (cut, mx, jnp.where(half == 1, zup[2], zdown[2]))
 
     def send_own_z(c):
-        dev = (cut, mx, jnp.where(p == 1, zup[2], zdown[2]))
         dst = jnp.where(p == 1, 0, H + R)
-        send(E.at[c, xi, rows(lo)], E.at[c, xi, rows(dst)], z_at[c], z_at[c], dev)
+        send(E.at[c, xi, rows(lo)], E.at[c, xi, rows(dst)], sz + c, rz + 4 * c, z_dev(p))
 
     def send_rest_z(c):
-        dev = (cut, mx, jnp.where(q == 1, zup[2], zdown[2]))
-        for k in range(2):
-            src = jnp.where(q == 1, H + R - 1 - k, H + k)
-            dst = jnp.where(q == 1, H - 1 - k, H + R + k)
-            send(E.at[c, xi, src], E.at[c, xi, dst], z_at[c] + 1 + k, z_at[c] + 1 + k, dev)
-
-    def send_x(c, base, at):
-        send(E.at[c, pl.ds(X, H), rows(at)], E.at[c, pl.ds(0, H), rows(at)], base, base, xup)
-        send(E.at[c, pl.ds(H, H), rows(at)], E.at[c, pl.ds(H + X, H), rows(at)], base + 1, base + 1, xdown)
-
-    def got_x(c, base, at):
-        arrived(E.at[c, pl.ds(0, H), rows(at)], base)
-        arrived(E.at[c, pl.ds(H + X, H), rows(at)], base + 1)
+        src = [jnp.where(q == 1, H + R - 1 - k, H + k) for k in range(2)]
+        dst = [jnp.where(q == 1, H - 1 - k, H + R + k) for k in range(2)]
+        for x in (H, H + X - 1):
+            send(E.at[c, x, src[0]], E.at[c, x, dst[0]], sz + c, rz + 4 * c + 1, z_dev(q))
+        send(E.at[c, mid, src[0]], E.at[c, mid, dst[0]], sz + c, rz + 4 * c + 2, z_dev(q))
+        send(E.at[c, xi, src[1]], E.at[c, xi, dst[1]], sz + c, rz + 4 * c + 3, z_dev(q))
+
+    def send_x(c, at):
+        send(E.at[c, pl.ds(X, H), rows(at)], E.at[c, pl.ds(0, H), rows(at)], sx + c, rx + c, xup)
+        send(E.at[c, pl.ds(H, H), rows(at)], E.at[c, pl.ds(H + X, H), rows(at)], sx + c, rx + c, xdown)
+
+    def got_x(c):
+        arrived(E.at[c, pl.ds(0, 4 * H), rows(0)], rx + c)
 
     def send_o(half):
         side = 1 - half
-        dev = (cut, mx, jnp.where(half == 1, zup[2], zdown[2]))
         src = jnp.where(half == 1, H + R - 1, H)
         dst = jnp.where(half == 1, 1, H + R)
-        send(O.at[xi, src], O.at[xi, dst], o_z + side, o_z + side, dev)
+        send(O.at[xi, src], O.at[xi, dst], so + 1 + side, ro + 1 + side, z_dev(half))
 
     own = pl.ds(H, R)
 
     def relay_o():
-        arrived(O.at[xi, rows(lq)], o_y)
+        arrived(O.at[xi, rows(lq)], ro)
         send_o(q)
-        send(O.at[H + X - 1, own], O.at[H - 1, own], o_x, o_x, xup)
-        send(O.at[H, own], O.at[H + X, own], o_x + 1, o_x + 1, xdown)
+        send(O.at[H + X - 1, own], O.at[H - 1, own], so + 3, ro + 3, xup)
+        send(O.at[H, own], O.at[H + X, own], so + 4, ro + 4, xdown)
 
     level_load.wait()
     for x in range(X):
@@ -202,11 +195,11 @@
     stage_away(0)
     stage_kept(0)
     pl.semaphore_wait(barrier, greeted)
-    send(O.at[xi, rows(lo)], O.at[xi, rows(lo)], o_y, o_y, yp)
+    send(O.at[xi, rows(lo)], O.at[xi, rows(lo)], so, ro, yp)
     send_y(0)
     send_o(p)
     send_own_z(0)
-    send_x(0, xo_at[0], lo)
+    send_x(0, lo)
     for c in range(1, S):
         stage_away(c)
         send_y(c)
@@ -215,18 +208,18 @@
             relay_o()
         if c < S - 1:
             send_own_z(c)
-        send_x(c, xo_at[c], lo)
+        send_x(c, lo)
     bound_load.wait()
     ritz_load.wait()
     for s in range(count):
         for x in range(X):
             for r in range(Y):
                 RA[s + 1, x, r] = ritz[s, pl.ds(x * Y + r, NR, stride=J), :]
-    send(RA.at[count], RA.at[0], c_at, c_at, cup)
-    send(RA.at[1], RA.at[count + 1], c_at + 1, c_at + 1, cdown)
-
-    arrived(RA.at[0], c_at)
-    arrived(RA.at[count + 1], c_at + 1)
+    send(RA.at[count], RA.at[0], sc, rc, cup)
+    send(RA.at[1], RA.at[count + 1], sc, rc + 1, cdown)
+
+    arrived(RA.at[0], rc)
+    arrived(RA.at[count + 1], rc + 1)
 
     @pl.when(cut == 0)
     def _():
@@ -236,16 +229,14 @@
     def _():
         RA[count + 1] = jnp.zeros((X, Y, NR, NZ), F32)
 
-    order = []
+    fresh = [[j for j in (c, c + 2) if j >= 2 or c < 2] for c in range(S)]
+    fresh = [[j for j in js if j not in sum(fresh[:c], [])] for c, js in enumerate(fresh)]
     for c in range(S):
-        for j in (c, c + 2):
-            if j not in order:
-                order.append(j)
-    for j in order:
-        send(RA.at[q * S + j], RQ.at[j], r_at + j, r_at + j, yp)
+        for j in fresh[c]:
+            send(RA.at[q * S + j], RQ.at[j], sr, rr + c, yp)
 
     def got_y(c):
-        arrived(E.at[c, xi, rows(lq)], y_at[c])
+        arrived(E.at[c, xi, rows(lq)], ry + c)
 
     last = R + 2 * H - 1
     ra = [a + p * (last - 2 * a) for a in range(last + 1)]
@@ -278,31 +269,29 @@
         return one, two
 
     def corners(c, a, k):
-        send(E.at[c, H + X - 1, ra[a]], E.at[c, H - 1, ra[a]], k, k, xup)
-        send(E.at[c, H, ra[a]], E.at[c, H + X, ra[a]], k + 1, k + 1, xdown)
-
-    def got_corners(c, a, k):
-        arrived(E.at[c, H - 1, ra[a]], k)
-        arrived(E.at[c, H + X, ra[a]], k + 1)
+        send(E.at[c, H + X - 1, ra[a]], E.at[c, H - 1, ra[a]], sk + c, rk + k, xup)
+        send(E.at[c, H, ra[a]], E.at[c, H + X, ra[a]], sk + c, rk + k, xdown)
+
+    def got_corners(c, k):
+        arrived(E.at[c, pl.ds(0, 2), 0], rk + k)
 
     def early_corners(c):
-        arrived(E.at[c, xi, rows(jnp.where(p == 1, 0, H + R))], z_at[c])
-        corners(c, far, k_at[c])
+        arrived(E.at[c, xi, rows(jnp.where(p == 1, 0, H + R))], rz + 4 * c)
+        corners(c, far, 2 * c)
 
     def late_corners(c):
-        arrived(E.at[c, xi, ra[near]], z_at[c] + 1)
-        corners(c, near, k_at[c] + 2)
+        arrived(E.at[c, pl.ds(0, 2), 0], rz + 4 * c + 1)
+        corners(c, near, 2 * c + 1)
 
     def got_o():
-        arrived(O.at[xi, H - 1], o_z)
-        arrived(O.at[xi, H + R], o_z + 1)
-        arrived(O.at[H - 1, own], o_x)
-        arrived(O.at[H + X, own], o_x + 1)
+        arrived(O.at[xi, H - 1], ro + 1)
+        arrived(O.at[xi, H + R], ro + 2)
+        arrived(O.at[H - 1, own], ro + 3)
+        arrived(O.at[H + X, own], ro + 4)
 
     def early(c):
         one, two = refs(c)
-        got_x(c, xo_at[c], lo)
-        got_x(c, xp_at[c], lq)
+        got_x(c)
         if c == 0:
             got_o()
 
@@ -310,14 +299,14 @@
             for a in range(H + 1, far + 1):
                 one(H + 1 + i, a)
 
-        loop(X - 2, 2, inner)
+        loop(X - 2, 6, inner)
         for x in (H, H + X - 1):
             for a in range(H + 1, far):
                 one(x, a)
         for x in (H - 1, H + X):
             for a in range(H + 1, far - 1):
                 one(x, a)
-        got_corners(c, far, k_at[c])
+        got_corners(c, 2 * c)
         for x in (H, H + X - 1):
             one(x, far)
         for x in (H - 1, H + X):
@@ -327,38 +316,39 @@
             for a in range(H + Y, far):
                 FT[c, i, ra[a] - lq] = two(H + i, a)
 
-        loop(X, 2, outer)
-        send(FT.at[c], FA.at[p * S + c], f_at[c], f_at[c], yp)
-
-    def late(c):
+        loop(X, 8, outer)
+        send(FT.at[c], FA.at[p * S + c], sf, rf + c, yp)
+
+    def row_gram(c, a, two, acc):
+        s, r = p * S + c, ra[a] - lo
+        for i in range(0, X, 2):
+            z = []
+            for x in (i, i + 1):
+                f = two(H + x, a)
+                FA[s, x, r] = f
+                z.append(jnp.concatenate([f, RA[s, x, r], RA[s + 2, x, r]], 0))
+            acc = acc + square(z)
+        return acc
+
+    def late_near(c):
         one, two = refs(c)
-        arrived(E.at[c, xi, ra[near - 1]], z_at[c] + 2)
-
-        def inner(i):
-            for a in (near, H):
-                one(H + 1 + i, a)
-
-        loop(X - 2, 2, inner)
-        for x in (H, H + X - 1):
+        arrived(E.at[c, mid, ra[near]], rz + 4 * c + 2)
+        for x in range(H, H + X):
             one(x, H)
-        got_corners(c, near, k_at[c] + 2)
+        for a in range(H + 1, H + Y):
+            GS[c] = row_gram(c, a, two, GS[c])
+
+    def late_far(c):
+        one, two = refs(c)
+        arrived(E.at[c, xi, ra[near - 1]], rz + 4 * c + 3)
+        for x in range(H + 1, H + X - 1):
+            one(x, near)
+        got_corners(c, 2 * c + 1)
         for x in (H, H + X - 1):
             one(x, near)
         for x in (H - 1, H + X):
             one(x, H)
-
-        s = p * S + c
-
-        def outer(i, acc):
-            for k in range(2):
-                x = 2 * i + k
-                for a in range(H, H + Y):
-                    FA[s, x, ra[a] - lo] = two(H + x, a)
-                z = [jnp.concatenate([FA[s, x, r], RA[s, x, r], RA[s + 2, x, r]], 0) for r in range(Y)]
-                acc = acc + square(z)
-            return acc
-
-        gram_pack(c, lax.fori_loop(0, X // 2, outer, GS[c]))
+        gram_pack(c, row_gram(c, H, two, GS[c]))
 
     def square(z):
         hi, lw = split(jnp.concatenate(z, 1))
@@ -366,18 +356,16 @@
 
     def product(f, w0, w1):
         def body(i, acc):
-            for k in range(2):
-                z = [jnp.concatenate([f(2 * i + k, r), w0(2 * i + k, r), w1(2 * i + k, r)], 0) for r in range(Y)]
+            for k in range(8):
+                x = 8 * i + k
+                z = [jnp.concatenate([f(x, r), w0(x, r), w1(x, r)], 0) for r in range(Y)]
                 acc = acc + square(z)
             return acc
 
-        return lax.fori_loop(0, X // 2, body, jnp.zeros((2 * NB, NB), F32))
+        return lax.fori_loop(0, X // 8, body, jnp.zeros((2 * NB, NB), F32))
 
     def gram_rest(c):
-        for j in (c, c + 2):
-            if j not in seen:
-                arrived(RQ.at[j], r_at + j)
-                seen.add(j)
+        arrived(RQ.at[pl.ds(0, len(fresh[c]))], rr + c)
         GS[c] = product(lambda x, r: FT[c, x, r], lambda x, r: RQ[c, x, r], lambda x, r: RQ[c + 2, x, r])
 
     def gram_pack(c, g):
@@ -399,15 +387,13 @@
         PK[c, 0] = t0
         PK[c, 1] = t1
 
-    seen = set()
-
     def spread(k, src):
         cs = groups[k]
         part = pl.ds(cs[0], len(cs))
         for o in range(1, span):
             t = lax.rem(me + o, span)
             x, z = (t // K, lax.rem(t, K)) if direct else (mx, t)
-            send(src.at[part], RZ.at[me, part], az_at[k] + o, az_at[k] + me, (cut, x, z * 2 + p))
+            send(src.at[part], RZ.at[me, part], sa + k, ra_ + k, (cut, x, z * 2 + p))
 
     def sum_start(k):
         cs = groups[k]
@@ -421,16 +407,14 @@
             spread(k, PK)
             return
         for o in range(1, nx):
-            send(PK.at[part], RX.at[mx, part], ax_at[k] + o, ax_at[k] + mx, (cut, lax.rem(mx + o, nx), my))
+            send(PK.at[part], RX.at[mx, part], sb + k, rb + k, (cut, lax.rem(mx + o, nx), my))
 
     def sum_more(k):
         if direct:
             return
         cs = groups[k]
         part = pl.ds(cs[0], len(cs))
-        for o in range(1, nx):
-            t = lax.rem(mx + o, nx)
-            arrived(RX.at[t, part], ax_at[k] + t)
+        arrived(RX.at[pl.ds(0, nx - 1), part], rb + k)
         for c in cs:
             acc = RX[0, c]
             for t in range(1, nx):
@@ -489,9 +473,7 @@
     def factor(k):
         cs = groups[k]
         part = pl.ds(cs[0], len(cs))
-        for o in range(1, span):
-            t = lax.rem(me + o, span)
-            arrived(RZ.at[t, part], az_at[k] + t)
+        arrived(RZ.at[pl.ds(0, span - 1), part], ra_ + k)
         both = [cleaned(c) for c in cs]
         mats = [m for m, _ in both]
         for j in range(0, NV, 2):
@@ -499,7 +481,7 @@
         mats = [scaled(m) for m in mats]
         for i, c in enumerate(cs):
             LP[c] = jnp.where(l32 < NB, mats[i], pltpu.roll(both[i][1], 2 * NV, 1))
-            send(LP.at[c], LR.at[c], l_at[c], l_at[c], yp)
+            send(LP.at[c], LR.at[c], sl, rl + c, yp)
         for i, c in enumerate(cs):
             LM[p * S + c] = mats[i][:, :NB]
             keep_corr(p * S + c, both[i][1])
@@ -509,11 +491,11 @@
 
     def take(c):
         s = q * S + c
-        arrived(LR.at[c], l_at[c])
+        arrived(LR.at[c], rl + c)
         wide = LR[c]
         LM[s] = wide[:, :NB]
         keep_corr(s, pltpu.roll(wide, 128 - 2 * NV, 1))
-        arrived(FA.at[s], f_at[c])
+        arrived(FA.at[s], rf + c)
 
     stored = []
 
@@ -533,7 +515,7 @@
             for r in range(Y):
                 out[s, pl.ds(x * Y + r, NV, stride=J), :] = o[:, r * NZ:(r + 1) * NZ]
 
-        loop(X, 2, body)
+        loop(X, 8, body)
         store(out.at[s], out_h.at[s], i)
 
     def finish_own(c):
@@ -542,28 +524,40 @@
     def finish_rest(c):
         take(c)
         finish(q * S + c, S + c)
+
+    def settle():
+        left(O.at[xi, rows(lo)], so)
+        for k in range(2):
+            left(O.at[xi, H], so + 1 + k)
+            left(O.at[H, own], so + 3 + k)
+        left(T, sy)
+        left(RQ, sr)
+        left(RA.at[pl.ds(0, 2)], sc)
+        for c in range(S):
+            left(E.at[c, xi, pl.ds(0, Y + 2)], sz + c)
+            left(E.at[c, pl.ds(0, 4 * H), rows(0)], sx + c)
+            left(E.at[c, pl.ds(0, 4), 0], sk + c)
 
     end = S - 1
     for c in range(S):
         got_y(c)
         send_rest_z(c)
-        send_x(c, xp_at[c], lq)
+        send_x(c, lq)
         if c == 0:
             send_own_z(end)
             early_corners(0)
         if c == 1:
             early_corners(1) if c < end else None
             early(0)
-            mark = len(pending)
     for c in range(2, end):
         early_corners(c)
     late_corners(0)
     for c in range(1, end):
         early(c)
     gram_rest(0)
-    late(0)
+    late_near(0)
     early_corners(end)
-    flush(mark // 2)
+    late_far(0)
     for c in range(1, end):
         gram_rest(c)
     early(end)
@@ -571,14 +565,16 @@
         late_corners(c)
     gram_rest(end)
     for c in range(1, end):
-        late(c)
+        late_near(c)
+        late_far(c)
     sum_start(0)
-    flush(mark - mark // 2)
     late_corners(end)
     sum_more(0)
-    late(end)
+    late_near(end)
+    late_far(end)
     sum_start(1)
     sum_more(1)
+    settle()
     factor(0)
     for c in range(end):
         finish_own(c)
@@ -586,13 +582,27 @@
     for c in range(end):
         finish_rest(c)
     finish_own(end)
-    flush(len(pending) - 1)
+    for k in range(2):
+        part = pl.ds(groups[k][0], len(groups[k]))
+        if not direct:
+            left(RX.at[pl.ds(0, nx - 1), part], sb + k)
+        left(RZ.at[pl.ds(0, span - 1), part], sa + k)
+    left(FT, sf)
     take(S - 1)
     store(cor, cor_h, 2 * S)
     finish(q * S + S - 1, 2 * S - 1)
     for copy in stored:
         copy.wait()
-    flush(len(pending))
+    left(LP, sl)
+
+
+def place(block, corr, block_out, corr_out, sem):
+    copies = [pltpu.make_async_copy(block.at[s], block_out.at[s], sem.at[s]) for s in range(block.shape[0])]
+    copies.append(pltpu.make_async_copy(corr, corr_out, sem.at[block.shape[0]]))
+    for copy in copies:
+        copy.start()
+    for copy in copies:
+        copy.wait()
 
 
 def on_device(disorder, slice_bounds, start, ritz):
@@ -605,7 +615,7 @@
     D = pltpu.SemaphoreType.DMA
     dims = (nc, nx, ny, count, NV, NR, X, Y, NZ)
     hbm = pl.BlockSpec(memory_space=pl.ANY)
-    sems = sem_counts(nx, K, S)
+    sends, receives = sem_counts(nx, K, S)
     block, corr = pl.pallas_call(
         functools.partial(kernel, dims),
         out_shape=(jax.ShapeDtypeStruct((count, NV * J, NZ), F32),
@@ -636,11 +646,19 @@
             V((count, NV, NV + 2 * NR), F32),
             V((S, NV, 128), F32),
             V((S, NV, 128), F32),
-            D((sems,)), D((sems,)),
+            D((sends,)), D((receives,)),
         ],
         compiler_params=pltpu.CompilerParams(collective_id=0, has_side_effects=True, vmem_limit_bytes=48 << 20),
     )(*[pltpu.with_memory_space_constraint(a, pltpu.HBM) for a in (
         disorder.reshape(J, NZ), slice_bounds.T, start.reshape(count, NV * J, NZ), ritz.reshape(count, NR * J, NZ))])
+    block, corr = pl.pallas_call(
+        place,
+        out_shape=(jax.ShapeDtypeStruct(block.shape, F32), jax.ShapeDtypeStruct(corr.shape, F32)),
+        in_specs=[hbm] * 2,
+        out_specs=(hbm, hbm),
+        scratch_shapes=[D((count + 1,))],
+        compiler_params=pltpu.CompilerParams(vmem_limit_bytes=1 << 20),
+    )(block, corr)
     return (block.reshape(start.shape), corr)
 
 

time: 59.3 us -> 56.3 us (0.949)
  local copies, waits for them, and re-layouts: 1.76 us -> 0 us
  Pallas kernels: 56.6 us -> 55.4 us
    pallas_call x1, Pallas kernels: 56.6 us -> 54.2 us  [on_device(): pl.pallas_call(functools.partial(kernel, dims), out_shape=(jax.ShapeDtype...]
    unnamed x2 -> x0, local copies, waits for them, and re-layouts: 1.76 us -> none
    pallas_call x0 -> x1, Pallas kernels: none -> 1.2 us  [on_device(): pl.pallas_call(place, out_shape=(jax.ShapeDtypeStruct(block.shape, F32),...]
where the time goes in v6:
time: 56.3 us; the launch traced here: 56 us
  Pallas kernels  55.4 us (98%)
  between operations  0.64 us (1%)
    pallas_call x1, Pallas kernels, on_device(): pl.pallas_call(functools.partial(kernel, dims), out_shape=(jax.ShapeDtype...  54.2 us
    pallas_call x1, Pallas kernels, on_device(): pl.pallas_call(place, out_shape=(jax.ShapeDtypeStruct(block.shape, F32),...  1.2 us

profile of v6, /device:TPU:0, one launch (start us, length us, event | category | flops | bytes accessed | tf_op | source)
XLA Modules:
  0.0 56.0 jit_solution(11731456565825914688)
XLA Ops:
  0.6 54.2 %shard_map.59 = (f32[6,512,128]{2,1,0:T(8,128)S(1)}, f32[6,16,32]{2,1,0:T(8,128)S(1)}) custom-call(s32[16,128]{1,0:T(8,128)} %bitcast.7, f32[2,6]{1,0:T(2,128)} %bitcast.8, f32[6,512,128]{2,1,0:T(8,128)} %bitcast.5, f32[6,128,128]{2,1,0:T(8,128)} %bitcast.6), custom_call_target="tpu_custom_call" | custom-call | tf_op jit(solution)/shard_map/pallas_call | solution.py:619
  54.8 1.2 %shard_map.60 = (f32[6,512,128]{2,1,0:T(8,128)}, f32[6,16,32]{2,1,0:T(8,128)}) custom-call(f32[6,512,128]{2,1,0:T(8,128)S(1)} %get-tuple-element.6.block, f32[6,16,32]{2,1,0:T(8,128)S(1)} %get-tuple-element.7.corr), custom_call_target="tpu_custom_call" | custom-call | tf_op jit(solution)/shard_map/pallas_call | solution.py:654

commit v7 on v6

--- a/solution.py
+++ b/solution.py
@@ -24,7 +24,7 @@
 
 def sem_counts(nx, K, S):
     more = 0 if direct_sum(nx, K) else 2
-    return 12 + 3 * S + more, 9 + 11 * S + more
+    return 13 + 3 * S + more, 10 + 11 * S + more
 
 
 def split(z):
@@ -44,7 +44,7 @@
 
 
 def kernel(dims, dis_h, bnd_h, start_h, ritz_h, out_h, cor_h, out, cor, bnd, dis, start, ritz, ls, E, T, O, U, FA, FT,
-           RA, RQ, GS, PK, RX, SM, RZ, LM, LP, LR, ss, rs):
+           RA, RQ, GS, GT, PK, RX, SM, RZ, LM, LP, LR, LC, LD, ss, rs):
     nc, nx, ny, count, NV, NR, X, Y, NZ = dims
     S = count // 2
     R = 2 * Y
@@ -90,11 +90,12 @@
     greet(cup)
     greet(cdown)
 
-    level_load = load(dis_h, dis, 2 * S)
     away, kept = [], []
     for c in range(S):
+        kept.append(load(start_h.at[p * S + c], start.at[S + c], S + c))
+        if c == 0:
+            level_load = load(dis_h, dis, 2 * S)
         away.append(load(start_h.at[q * S + c], start.at[c], c))
-        kept.append(load(start_h.at[p * S + c], start.at[S + c], S + c))
     bound_load = load(bnd_h, bnd, 2 * S + 2)
     ritz_load = load(ritz_h, ritz, 2 * S + 1)
 
@@ -138,9 +139,9 @@
     def rows(at):
         return pl.ds(at, Y)
 
-    so, sy, sf, sl, sr, sc = (take_slots(0, n) for n in (5, 1, 1, 1, 1, 1))
+    so, sy, sf, sl, sr, sc, sd = (take_slots(0, n) for n in (5, 1, 1, 1, 1, 1, 1))
     sz, sx, sk, sa = (take_slots(0, n) for n in (S, S, S, 2))
-    ro, ry, rf, rl, rx, rc, rr, ra_ = (take_slots(1, n) for n in (5, S, S, S, S, 2, S, 2))
+    ro, ry, rf, rl, rx, rc, rr, ra_, rd = (take_slots(1, n) for n in (5, S, S, S, S, 2, S, 2, 1))
     rz, rk = take_slots(1, 4 * S), take_slots(1, 2 * S)
     groups = [list(range(S - 1)), [S - 1]]
     direct = direct_sum(nx, K)
@@ -192,13 +193,13 @@
         for r in range(Y):
             row = dis[pl.ds(x * Y + r, 1), :].astype(F32)
             O[H + x, lo + r] = 16.5 * (row / F32(LEVELS - 1) - 0.5)
-    stage_away(0)
     stage_kept(0)
     pl.semaphore_wait(barrier, greeted)
     send(O.at[xi, rows(lo)], O.at[xi, rows(lo)], so, ro, yp)
-    send_y(0)
     send_o(p)
     send_own_z(0)
+    stage_away(0)
+    send_y(0)
     send_x(0, lo)
     for c in range(1, S):
         stage_away(c)
@@ -319,7 +320,7 @@
         loop(X, 8, outer)
         send(FT.at[c], FA.at[p * S + c], sf, rf + c, yp)
 
-    def row_gram(c, a, two, acc):
+    def row_gram(c, a, two, acc, product=None):
         s, r = p * S + c, ra[a] - lo
         for i in range(0, X, 2):
             z = []
@@ -327,7 +328,7 @@
                 f = two(H + x, a)
                 FA[s, x, r] = f
                 z.append(jnp.concatenate([f, RA[s, x, r], RA[s + 2, x, r]], 0))
-            acc = acc + square(z)
+            acc = acc + (product or square)(z)
         return acc
 
     def late_near(c):
@@ -335,8 +336,12 @@
         arrived(E.at[c, mid, ra[near]], rz + 4 * c + 2)
         for x in range(H, H + X):
             one(x, H)
+        g = GS[c]
         for a in range(H + 1, H + Y):
-            GS[c] = row_gram(c, a, two, GS[c])
+            g = row_gram(c, a, two, g)
+        g = jnp.concatenate([g, jnp.zeros((2 * NB, 128 - NB), F32)], 1)
+        cross = jnp.concatenate([g[NB:], jnp.zeros((128 - NB, 128), F32)], 0)
+        GT[c] = g[:NB] + (cross + cross.T)[:NB]
 
     def late_far(c):
         one, two = refs(c)
@@ -348,11 +353,17 @@
             one(x, near)
         for x in (H - 1, H + X):
             one(x, H)
-        gram_pack(c, row_gram(c, H, two, GS[c]))
+        g = row_gram(c, H, two, jnp.zeros((NB, NB), F32), symmetric)
+        gram_pack(c, GT[c] + jnp.concatenate([g, jnp.zeros((NB, 128 - NB), F32)], 1))
 
     def square(z):
         hi, lw = split(jnp.concatenate(z, 1))
         return lax.dot_general(jnp.concatenate([hi, lw], 0), hi, NT, preferred_element_type=F32)
+
+    def symmetric(z):
+        hi, lw = split(jnp.concatenate(z, 1))
+        a = lax.dot_general(jnp.concatenate([hi, lw], 0), hi, NT, preferred_element_type=F32)
+        return a[:NB] + a[NB:] + lax.dot_general(hi, lw, NT, preferred_element_type=F32)
 
     def product(f, w0, w1):
         def body(i, acc):
@@ -369,9 +380,6 @@
         GS[c] = product(lambda x, r: FT[c, x, r], lambda x, r: RQ[c, x, r], lambda x, r: RQ[c + 2, x, r])
 
     def gram_pack(c, g):
-        g = jnp.concatenate([g, jnp.zeros((2 * NB, 128 - NB), F32)], 1)
-        cross = jnp.concatenate([g[NB:], jnp.zeros((128 - NB, 128), F32)], 0)
-        g = g[:NB] + (cross + cross.T)[:NB]
         lane = lax.broadcasted_iota(jnp.int32, (8, 128), 1)
         t0 = jnp.zeros((8, 128), F32)
         t1 = jnp.zeros((8, 128), F32)
@@ -430,7 +438,6 @@
     eye = jnp.where(l32 == r32 + NV, 1.0, 0.0)
 
     line = lax.broadcasted_iota(jnp.int32, (NV, 1), 0)
-    odd = r32 % 2
 
     def strip(t, at):
         return pltpu.roll(t, 128 - at, 1) if at else t
@@ -450,41 +457,53 @@
         sub = lax.dot_general(fb, fn, NT, precision=HP, preferred_element_type=F32)
         sub = jnp.concatenate([sub, jnp.zeros((NV, 128 - NV), F32)], 1)
         wide = jnp.where(l32 < NW, fw, 0.0)
-        return jnp.where(l32 < NV, ff - sub, eye) - pltpu.roll(wide, 2 * NV, 1), wide
-
-    def eliminate(M, j):
-        r0, r1 = M[j:j + 1], M[j + 1:j + 2]
-        c0 = jnp.broadcast_to(M[:, j:j + 1], (NV, 128))
-        c1 = jnp.broadcast_to(M[:, j + 1:j + 2], (NV, 128))
-        p00, p01, p11 = c0[j:j + 1], c1[j:j + 1], c1[j + 1:j + 2]
+        return jnp.where(l32 < NV, ff - sub, eye) - pltpu.roll(wide, 2 * NV, 1), t1
+
+    def pair(a, b, i, scale, ratio):
+        p00, p01, p11 = a[i:i + 1], b[i:i + 1], b[i + 1:i + 2]
         inv = 1.0 / (p00 * p11 - p01 * p01)
-        g0 = (p11 * r0 - p01 * r1) * inv
-        g1 = (p00 * r1 - p01 * r0) * inv
-        return jnp.where(line > j + 1, M - c0 * g0 - c1 * g1, M)
-
-    def scaled(M):
-        diag = jnp.sum(jnp.where(l32 == r32, M, 0.0), axis=1, keepdims=True)
-        side = jnp.sum(jnp.where(l32 == r32 - odd, M, 0.0), axis=1, keepdims=True)
-        ratio = side / pltpu.roll(jnp.broadcast_to(diag, (NV, 128)), 1, 0)
-        M = jnp.where(odd == 1, M - ratio * pltpu.roll(M, 1, 0), M)
-        diag = jnp.sum(jnp.where(l32 == r32, M, 0.0), axis=1, keepdims=True)
-        return pltpu.roll(M * (1.0 / jnp.sqrt(diag)), 128 - NV, 1)
+        scale = jnp.where(line == i, 1.0 / jnp.sqrt(p00), jnp.where(line == i + 1, jnp.sqrt(p00 * inv), scale))
+        ratio = jnp.where(line == i + 1, p01 / p00, ratio)
+        return (lambda u, v: ((p11 * u - p01 * v) * inv, (p00 * v - p01 * u) * inv)), scale, ratio
+
+    def eliminate(state, j):
+        M, scale, ratio = state
+        c = [jnp.broadcast_to(M[:, j + k:j + k + 1], (NV, 128)) for k in range(4)]
+        r = [M[j + k:j + k + 1] for k in range(4)]
+        solve, scale, ratio = pair(c[0], c[1], j, scale, ratio)
+        g0, g1 = solve(r[0], r[1])
+        for k in (2, 3):
+            h0, h1 = solve(c[k][j:j + 1], c[k][j + 1:j + 2])
+            r[k] = r[k] - c[0][j + k:j + k + 1] * g0 - c[1][j + k:j + k + 1] * g1
+            c[k] = c[k] - c[0] * h0 - c[1] * h1
+        solve, scale, ratio = pair(c[2], c[3], j + 2, scale, ratio)
+        g2, g3 = solve(r[2], r[3])
+        M = jnp.where(line > j + 1, M - c[0] * g0 - c[1] * g1, M)
+        return jnp.where(line > j + 3, M - c[2] * g2 - c[3] * g3, M), scale, ratio
+
+    def scaled(state):
+        M, scale, ratio = state
+        return pltpu.roll((M - ratio * pltpu.roll(M, 1, 0)) * scale, 128 - NV, 1)
 
     def factor(k):
         cs = groups[k]
-        part = pl.ds(cs[0], len(cs))
-        arrived(RZ.at[pl.ds(0, span - 1), part], ra_ + k)
+        arrived(RZ.at[pl.ds(0, span - 1), pl.ds(cs[0], len(cs))], ra_ + k)
         both = [cleaned(c) for c in cs]
-        mats = [m for m, _ in both]
-        for j in range(0, NV, 2):
+        blank = jnp.zeros((NV, 128), F32)
+        mats = [(m, blank, blank) for m, _ in both]
+        for j in range(0, NV, 4):
             mats = [eliminate(m, j) for m in mats]
         mats = [scaled(m) for m in mats]
         for i, c in enumerate(cs):
-            LP[c] = jnp.where(l32 < NB, mats[i], pltpu.roll(both[i][1], 2 * NV, 1))
+            low = jnp.where(l32 < NB, mats[i], 0.0)
+            LP[c] = low[:NV // 2] + pltpu.roll(low[NV // 2:], 64, 1)
             send(LP.at[c], LR.at[c], sl, rl + c, yp)
         for i, c in enumerate(cs):
+            LC[c] = both[i][1]
             LM[p * S + c] = mats[i][:, :NB]
-            keep_corr(p * S + c, both[i][1])
+
+    def unpacked(t1):
+        return jnp.where(l32 < NW, jnp.concatenate([strip(t1, b * NW) for b in range(NV // 8)], 0), 0.0)
 
     def keep_corr(s, wide):
         cor[s] = jnp.concatenate([wide, jnp.zeros((128 - NV, 128), F32)], 0).T[:NW, :NV]
@@ -492,9 +511,8 @@
     def take(c):
         s = q * S + c
         arrived(LR.at[c], rl + c)
-        wide = LR[c]
-        LM[s] = wide[:, :NB]
-        keep_corr(s, pltpu.roll(wide, 128 - 2 * NV, 1))
+        half = LR[c]
+        LM[s] = jnp.concatenate([half, pltpu.roll(half, 64, 1)], 0)[:, :NB]
         arrived(FA.at[s], rf + c)
 
     stored = []
@@ -576,24 +594,29 @@
     sum_more(1)
     settle()
     factor(0)
-    for c in range(end):
+    factor(1)
+    send(LC, LD, sd, rd, yp)
+    for c in range(S):
         finish_own(c)
-    factor(1)
-    for c in range(end):
-        finish_rest(c)
-    finish_own(end)
     for k in range(2):
         part = pl.ds(groups[k][0], len(groups[k]))
         if not direct:
             left(RX.at[pl.ds(0, nx - 1), part], sb + k)
         left(RZ.at[pl.ds(0, span - 1), part], sa + k)
     left(FT, sf)
-    take(S - 1)
+    for c in range(end):
+        finish_rest(c)
+    for c in range(S):
+        keep_corr(p * S + c, unpacked(LC[c]))
+    finish_rest(end)
+    arrived(LD, rd)
+    for c in range(S):
+        keep_corr(q * S + c, unpacked(LD[c]))
     store(cor, cor_h, 2 * S)
-    finish(q * S + S - 1, 2 * S - 1)
     for copy in stored:
         copy.wait()
     left(LP, sl)
+    left(LC, sd)
 
 
 def place(block, corr, block_out, corr_out, sem):
@@ -639,13 +662,16 @@
             V((count + 2, X, Y, NR, NZ), F32),
             V((S + 2, X, Y, NR, NZ), F32),
             V((S, 2 * (NV + 2 * NR), NV + 2 * NR), F32),
+            V((S, NV + 2 * NR, 128), F32),
             V((S, 2, 8, 128), F32),
             V((nx, S, 2, 8, 128), F32),
             V((S, 2, 8, 128), F32),
             V((nx * K if direct_sum(nx, K) else K, S, 2, 8, 128), F32),
             V((count, NV, NV + 2 * NR), F32),
-            V((S, NV, 128), F32),
-            V((S, NV, 128), F32),
+            V((S, NV // 2, 128), F32),
+            V((S, NV // 2, 128), F32),
+            V((S, 8, 128), F32),
+            V((S, 8, 128), F32),
             D((sends,)), D((receives,)),
         ],
         compiler_params=pltpu.CompilerParams(collective_id=0, has_side_effects=True, vmem_limit_bytes=48 << 20),

time: 56.3 us -> 55.6 us (0.988)
  no operation moved by 1% of the time
where the time goes in v7:
time: 55.6 us; the launch traced here: 55.5 us
  Pallas kernels  54.9 us (99%)
  between operations  0.64 us (1%)
    pallas_call x1, Pallas kernels, on_device(): pl.pallas_call(functools.partial(kernel, dims), out_shape=(jax.ShapeDtype...  53.7 us
    pallas_call x1, Pallas kernels, on_device(): pl.pallas_call(place, out_shape=(jax.ShapeDtypeStruct(block.shape, F32),...  1.2 us

profile of v7, /device:TPU:0, one launch (start us, length us, event | category | flops | bytes accessed | tf_op | source)
XLA Modules:
  0.0 55.5 jit_solution(15838866259156254354)
XLA Ops:
  0.6 53.7 %shard_map.59 = (f32[6,512,128]{2,1,0:T(8,128)S(1)}, f32[6,16,32]{2,1,0:T(8,128)S(1)}) custom-call(s32[16,128]{1,0:T(8,128)} %bitcast.7, f32[2,6]{1,0:T(2,128)} %bitcast.8, f32[6,512,128]{2,1,0:T(8,128)} %bitcast.5, f32[6,128,128]{2,1,0:T(8,128)} %bitcast.6), custom_call_target="tpu_custom_call" | custom-call | tf_op jit(solution)/shard_map/pallas_call | solution.py:642
  54.3 1.2 %shard_map.60 = (f32[6,512,128]{2,1,0:T(8,128)}, f32[6,16,32]{2,1,0:T(8,128)}) custom-call(f32[6,512,128]{2,1,0:T(8,128)S(1)} %get-tuple-element.6.block, f32[6,16,32]{2,1,0:T(8,128)S(1)} %get-tuple-element.7.corr), custom_call_target="tpu_custom_call" | custom-call | tf_op jit(solution)/shard_map/pallas_call | solution.py:680

commit v8 on v7

--- a/solution.py
+++ b/solution.py
@@ -457,7 +457,12 @@
         sub = lax.dot_general(fb, fn, NT, precision=HP, preferred_element_type=F32)
         sub = jnp.concatenate([sub, jnp.zeros((NV, 128 - NV), F32)], 1)
         wide = jnp.where(l32 < NW, fw, 0.0)
-        return jnp.where(l32 < NV, ff - sub, eye) - pltpu.roll(wide, 2 * NV, 1), t1
+        square_of = jnp.where(l32 == r32, ff, 0.0)
+        by_row = 1.0 / jnp.sqrt(jnp.sum(square_of, axis=1, keepdims=True))
+        by_lane = jnp.sum(square_of, axis=0, keepdims=True)
+        by_lane = jnp.where(l32[:1] < NV, 1.0 / jnp.sqrt(by_lane), 1.0)
+        M = jnp.where(l32 < NV, ff - sub, eye) - pltpu.roll(wide, 2 * NV, 1)
+        return M * (by_row * by_lane), t1
 
     def pair(a, b, i, scale, ratio):
         p00, p01, p11 = a[i:i + 1], b[i:i + 1], b[i + 1:i + 2]

time: 55.6 us -> 55.7 us (level)
  no operation moved by 1% of the time
where the time goes in v8:
time: 55.7 us; the launch traced here: 55.5 us
  Pallas kernels  54.9 us (99%)
  between operations  0.64 us (1%)
    pallas_call x1, Pallas kernels, on_device(): pl.pallas_call(functools.partial(kernel, dims), out_shape=(jax.ShapeDtype...  53.7 us
    pallas_call x1, Pallas kernels, on_device(): pl.pallas_call(place, out_shape=(jax.ShapeDtypeStruct(block.shape, F32),...  1.2 us

profile of v8, /device:TPU:0, one launch (start us, length us, event | category | flops | bytes accessed | tf_op | source)
XLA Modules:
  0.0 55.5 jit_solution(8215282306755122844)
XLA Ops:
  0.6 53.7 %shard_map.59 = (f32[6,512,128]{2,1,0:T(8,128)S(1)}, f32[6,16,32]{2,1,0:T(8,128)S(1)}) custom-call(s32[16,128]{1,0:T(8,128)} %bitcast.7, f32[2,6]{1,0:T(2,128)} %bitcast.8, f32[6,512,128]{2,1,0:T(8,128)} %bitcast.5, f32[6,128,128]{2,1,0:T(8,128)} %bitcast.6), custom_call_target="tpu_custom_call" | custom-call | tf_op jit(solution)/shard_map/pallas_call | solution.py:647
  54.3 1.2 %shard_map.60 = (f32[6,512,128]{2,1,0:T(8,128)}, f32[6,16,32]{2,1,0:T(8,128)}) custom-call(f32[6,512,128]{2,1,0:T(8,128)S(1)} %get-tuple-element.6.block, f32[6,16,32]{2,1,0:T(8,128)S(1)} %get-tuple-element.7.corr), custom_call_target="tpu_custom_call" | custom-call | tf_op jit(solution)/shard_map/pallas_call | solution.py:685

commit v9 on v8

--- a/solution.py
+++ b/solution.py
@@ -398,9 +398,16 @@
     def spread(k, src):
         cs = groups[k]
         part = pl.ds(cs[0], len(cs))
+        bits = K.bit_length() - 1
+        flips = direct and K == 1 << bits
+        steps = [(dx, dz) for dz in reversed(range(K)) for dx in reversed(range(nx)) if dx or dz]
         for o in range(1, span):
             t = lax.rem(me + o, span)
             x, z = (t // K, lax.rem(t, K)) if direct else (mx, t)
+            if flips:
+                dx, dz = steps[o - 1]
+                x = lax.rem(mx + dx, nx)
+                z = sum(lax.rem(kz // (1 << b) + (dz >> b), 2) * (1 << b) for b in range(bits))
             send(src.at[part], RZ.at[me, part], sa + k, ra_ + k, (cut, x, z * 2 + p))
 
     def sum_start(k):

time: 55.7 us -> 55.5 us (level)
  no operation moved by 1% of the time
where the time goes in v9:
time: 55.5 us; the launch traced here: 55.3 us
  Pallas kernels  54.7 us (99%)
  between operations  0.64 us (1%)
    pallas_call x1, Pallas kernels, on_device(): pl.pallas_call(functools.partial(kernel, dims), out_shape=(jax.ShapeDtype...  53.5 us
    pallas_call x1, Pallas kernels, on_device(): pl.pallas_call(place, out_shape=(jax.ShapeDtypeStruct(block.shape, F32),...  1.2 us

profile of v9, /device:TPU:0, one launch (start us, length us, event | category | flops | bytes accessed | tf_op | source)
XLA Modules:
  0.0 55.3 jit_solution(4745023093827588599)
XLA Ops:
  0.6 53.5 %shard_map.59 = (f32[6,512,128]{2,1,0:T(8,128)S(1)}, f32[6,16,32]{2,1,0:T(8,128)S(1)}) custom-call(s32[16,128]{1,0:T(8,128)} %bitcast.7, f32[2,6]{1,0:T(2,128)} %bitcast.8, f32[6,512,128]{2,1,0:T(8,128)} %bitcast.5, f32[6,128,128]{2,1,0:T(8,128)} %bitcast.6), custom_call_target="tpu_custom_call" | custom-call | tf_op jit(solution)/shard_map/pallas_call | solution.py:654
  54.1 1.2 %shard_map.60 = (f32[6,512,128]{2,1,0:T(8,128)}, f32[6,16,32]{2,1,0:T(8,128)}) custom-call(f32[6,512,128]{2,1,0:T(8,128)S(1)} %get-tuple-element.6.block, f32[6,16,32]{2,1,0:T(8,128)S(1)} %get-tuple-element.7.corr), custom_call_target="tpu_custom_call" | custom-call | tf_op jit(solution)/shard_map/pallas_call | solution.py:692

commit v10 on v9

--- a/solution.py
+++ b/solution.py
@@ -24,7 +24,7 @@
 
 def sem_counts(nx, K, S):
     more = 0 if direct_sum(nx, K) else 2
-    return 13 + 3 * S + more, 10 + 11 * S + more
+    return 14 + 3 * S + more, 11 + 11 * S + more
 
 
 def split(z):
@@ -139,9 +139,9 @@
     def rows(at):
         return pl.ds(at, Y)
 
-    so, sy, sf, sl, sr, sc, sd = (take_slots(0, n) for n in (5, 1, 1, 1, 1, 1, 1))
+    so, sy, sf, sl, sr, sc, sd = (take_slots(0, n) for n in (5, 1, 1, 1, 1, 1, 2))
     sz, sx, sk, sa = (take_slots(0, n) for n in (S, S, S, 2))
-    ro, ry, rf, rl, rx, rc, rr, ra_, rd = (take_slots(1, n) for n in (5, S, S, S, S, 2, S, 2, 1))
+    ro, ry, rf, rl, rx, rc, rr, ra_, rd = (take_slots(1, n) for n in (5, S, S, S, S, 2, S, 2, 2))
     rz, rk = take_slots(1, 4 * S), take_slots(1, 2 * S)
     groups = [list(range(S - 1)), [S - 1]]
     direct = direct_sum(nx, K)
@@ -513,6 +513,8 @@
         for i, c in enumerate(cs):
             LC[c] = both[i][1]
             LM[p * S + c] = mats[i][:, :NB]
+        part = pl.ds(cs[0], len(cs))
+        send(LC.at[part], LD.at[part], sd + k, rd + k, yp)
 
     def unpacked(t1):
         return jnp.where(l32 < NW, jnp.concatenate([strip(t1, b * NW) for b in range(NV // 8)], 0), 0.0)
@@ -607,7 +609,6 @@
     settle()
     factor(0)
     factor(1)
-    send(LC, LD, sd, rd, yp)
     for c in range(S):
         finish_own(c)
     for k in range(2):
@@ -620,15 +621,18 @@
         finish_rest(c)
     for c in range(S):
         keep_corr(p * S + c, unpacked(LC[c]))
+    arrived(LD.at[pl.ds(0, end)], rd)
+    for c in range(end):
+        keep_corr(q * S + c, unpacked(LD[c]))
     finish_rest(end)
-    arrived(LD, rd)
-    for c in range(S):
-        keep_corr(q * S + c, unpacked(LD[c]))
+    arrived(LD.at[pl.ds(end, 1)], rd + 1)
+    keep_corr(q * S + end, unpacked(LD[end]))
     store(cor, cor_h, 2 * S)
     for copy in stored:
         copy.wait()
     left(LP, sl)
-    left(LC, sd)
+    left(LC.at[pl.ds(0, end)], sd)
+    left(LC.at[pl.ds(end, 1)], sd + 1)
 
 
 def place(block, corr, block_out, corr_out, sem):

time: 55.5 us -> 55.5 us (level)
  no operation moved by 1% of the time
where the time goes in v10:
time: 55.5 us; the launch traced here: 55.3 us
  Pallas kernels  54.7 us (99%)
  between operations  0.64 us (1%)
    pallas_call x1, Pallas kernels, on_device(): pl.pallas_call(functools.partial(kernel, dims), out_shape=(jax.ShapeDtype...  53.5 us
    pallas_call x1, Pallas kernels, on_device(): pl.pallas_call(place, out_shape=(jax.ShapeDtypeStruct(block.shape, F32),...  1.2 us

profile of v10, /device:TPU:0, one launch (start us, length us, event | category | flops | bytes accessed | tf_op | source)
XLA Modules:
  0.0 55.3 jit_solution(12378631624176191143)
XLA Ops:
  0.6 53.5 %shard_map.59 = (f32[6,512,128]{2,1,0:T(8,128)S(1)}, f32[6,16,32]{2,1,0:T(8,128)S(1)}) custom-call(s32[16,128]{1,0:T(8,128)} %bitcast.7, f32[2,6]{1,0:T(2,128)} %bitcast.8, f32[6,512,128]{2,1,0:T(8,128)} %bitcast.5, f32[6,128,128]{2,1,0:T(8,128)} %bitcast.6), custom_call_target="tpu_custom_call" | custom-call | tf_op jit(solution)/shard_map/pallas_call | solution.py:658
  54.1 1.2 %shard_map.60 = (f32[6,512,128]{2,1,0:T(8,128)}, f32[6,16,32]{2,1,0:T(8,128)}) custom-call(f32[6,512,128]{2,1,0:T(8,128)S(1)} %get-tuple-element.6.block, f32[6,16,32]{2,1,0:T(8,128)S(1)} %get-tuple-element.7.corr), custom_call_target="tpu_custom_call" | custom-call | tf_op jit(solution)/shard_map/pallas_call | solution.py:696
